TPU v7x, 128 devices: a whole 4x4x4 slice. The times are simulated.
128 devices in a mesh: seq: 8 (over y_lo, x), samp: 16 (over y_hi, z, core).
Axes of the slice: x: 4, y: 4 (y_hi: 2, y_lo: 2; y = y_hi * 2 + y_lo), z: 4, core: 2. Of those that a mesh axis runs over, the one named last changes fastest.
Arguments:
- prompt_ids: int32 [2048], replicated, may hold values from 0 to 64127
- comp_ids: int32 [64, 2], replicated, may hold values from 0 to 64127
- prefix_len: int32 [1], replicated, may hold values from 8192 to 16384
- prompt_offset: int32 [1], replicated, may hold values from 16384 to 32768
- embed_table: bfloat16 [64128, 8192], P('seq', 'samp'), may hold values from -3 to 3
- attn_gain: bfloat16 [8192], P('samp'), may hold values from 0.099609375 to 1.8984375
- query_key_value_weight: bfloat16 [8192, 10240], P('samp', 'seq')
- w_out: bfloat16 [8192, 8192], P('seq', 'samp'), may hold values from -0.29882812 to 0.29882812
- key_value_cache: bfloat16 [2, 8, 16384, 128], P(None, 'seq'), may hold values from -6 to 6
Outputs:
- prompt_out: bfloat16 [2048, 8192], P('seq', 'samp')
- comp_out: bfloat16 [64, 2, 8192], P('seq', None, 'samp')
Inputs may be any that keep to these rules, and one draw needn't show every extreme that they name: The valid cache slots are slots 0 to prefix_len - 1. The valid cache slots hold the positions directly before prompt_offset.
All inputs are finite; a program needn't handle non-finite values.
Results may differ from a plain program's by a relative error of at most 0.03.
Values may be sent and summed in bfloat16 or wider, within the bound.
No kernel may reach another device: no remote copies, remote signals or barrier semaphores. Data moves between devices by JAX's collectives and lax.ppermute only.
A program may use at most 192 MiB of HBM per device.

v0:
```python
import functools
import math

import jax
import jax.numpy as jnp
from jax import lax
from jax.experimental import pallas as pl
from jax.experimental.pallas import tpu as pltpu
from jax.sharding import PartitionSpec as P


NORM_EPS = 1e-05
MASK_FILL = -1e30
HEAD = 128
HEADS = 8
SEQ = 8
GROUPS = 8
SAMP = 16
ROWS = 136
PROMPT_ROWS = 128
FEATURES = 8192
LOG2_SCALE = math.log2(math.e) / math.sqrt(HEAD)
LAST_DIMS = (((1,), (1,)), ((), ()))

SAME_CORE = [[2 * g + c for g in range(GROUPS)] for c in range(2)]
SEQ_CORE = [[SAMP * s + 2 * g + c for s in range(SEQ) for c in range(2)] for g in range(GROUPS)]
SEQ_GROUP = [[SAMP * s + 2 * g + c for s in range(SEQ) for g in range(GROUPS)] for c in range(2)]
SHIFTS = ((0, 0), (0, 1), (1, 0), (1, 1), (3, 0), (3, 1), (2, 0), (2, 1))


def rope_freqs(head_dim):
    half_dim = head_dim // 2
    dim_index = jnp.arange(half_dim, dtype=jnp.float32)
    base_freq = 1.0 / jnp.power(500000.0, 2.0 * dim_index / head_dim)
    wavelength = 2.0 * math.pi / base_freq
    blend = (8192.0 / wavelength - 1.0) / 3.0
    middle = (1.0 - blend) * base_freq / 8.0 + blend * base_freq
    return jnp.where(
        wavelength > 8192.0, base_freq / 8.0, jnp.where(wavelength < 2048.0, base_freq, middle)
    )


def moved(index, shift, sign=1):
    return (index % 4 + sign * shift[0] + 4) % 4 + 4 * ((index // 4) ^ shift[1])


def to_seq(block, shift):
    return lax.ppermute(block, "seq", [(i, moved(i, shift)) for i in range(SEQ)])


def to_other_core(block):
    return lax.ppermute(block, "samp", [(i, i ^ 1) for i in range(SAMP)])


def exchange(blocks, axes, groups=None):
    return lax.all_to_all(blocks, axes, 0, 0, tiled=True, axis_index_groups=groups)


def whole(memory_space=pltpu.VMEM):
    return pl.BlockSpec(memory_space=memory_space)


def merge_kernel(place, got, owner, copies, kept, given, held, sem):
    core = place[1]
    halves = []
    for c in range(2):
        total = jnp.zeros(kept.shape, jnp.float32)
        for s in range(SEQ):
            total = jnp.where(owner[...] == s, got[2 * s + c].astype(jnp.float32), total)
        halves.append(total.astype(jnp.bfloat16))
    held[...] = jnp.concatenate(halves, axis=1)
    sends = [pltpu.make_async_copy(held, copies.at[s], sem.at[s]) for s in range(SEQ)]
    for send in sends:
        send.start()

    @pl.when(core == 0)
    def _():
        kept[...] = halves[0]
        given[...] = halves[1]

    @pl.when(core == 1)
    def _():
        kept[...] = halves[1]
        given[...] = halves[0]

    for send in sends:
        send.wait()


def merge(place, got, owner):
    width = got.shape[2]
    half = jax.ShapeDtypeStruct((ROWS, width), jnp.bfloat16)
    return pl.pallas_call(
        merge_kernel,
        out_shape=(pltpu.HBM((SEQ, ROWS, 2 * width), jnp.bfloat16), half, half),
        in_specs=[whole(pltpu.SMEM), whole(), whole()],
        out_specs=(whole(pltpu.HBM), whole(), whole()),
        scratch_shapes=[
            pltpu.VMEM((ROWS, 2 * width), jnp.bfloat16),
            pltpu.SemaphoreType.DMA((SEQ,)),
        ],
        compiler_params=pltpu.CompilerParams(vmem_limit_bytes=16 << 20),
        name="merge",
    )(place, got, owner)


def project_kernel(place, rows, w_own, w_other, out, comp, weights, held, sem):
    core = place[1]
    depth, width = w_own.shape
    weights[pl.ds(pl.multiple_of(core * depth, depth), depth), :] = w_own[...]
    weights[pl.ds(pl.multiple_of((1 - core) * depth, depth), depth), :] = w_other[...]
    gathered = jnp.concatenate([rows[s, PROMPT_ROWS:, :] for s in range(SEQ)], axis=0)
    n = SEQ * GROUPS
    to_row = lax.broadcasted_iota(jnp.int32, (n, n), 0)
    from_row = lax.broadcasted_iota(jnp.int32, (n, n), 1)
    wanted = (to_row % SEQ) * GROUPS + to_row // SEQ
    order = jnp.where(from_row == wanted, 1.0, 0.0).astype(jnp.bfloat16)
    comp[...] = jnp.dot(order, gathered, preferred_element_type=jnp.float32)

    def send(g):
        return pltpu.make_async_copy(held.at[g], out.at[g], sem.at[g])

    def block_of(g, carry):
        parts = [rows[s, pl.ds(pl.multiple_of(16 * g, 16), 16), :] for s in range(SEQ)]
        parts.append(comp[pl.ds(pl.multiple_of(8 * g, 8), 8), :].astype(jnp.bfloat16))
        block = jnp.concatenate(parts, axis=0)
        product = jnp.dot(block, weights[...], preferred_element_type=jnp.float32)
        wide = block.astype(jnp.float32)
        squares = jnp.sum(wide * wide, axis=1, keepdims=True)
        high = squares.astype(jnp.bfloat16).astype(jnp.float32)
        lane = lax.broadcasted_iota(jnp.int32, (ROWS, HEAD), 1)
        extra = jnp.where(lane == 0, high, jnp.where(lane == 1, squares - high, 0.0))
        held[g, :, :width] = product.astype(jnp.bfloat16)
        held[g, :, width:] = extra.astype(jnp.bfloat16)
        send(g).start()
        return carry

    lax.fori_loop(0, GROUPS, block_of, 0)
    for g in range(GROUPS):
        send(g).wait()


def project(place, rows, w_own, w_other):
    depth, width = w_own.shape
    return pl.pallas_call(
        project_kernel,
        out_shape=pltpu.HBM((GROUPS, ROWS, width + HEAD), jnp.bfloat16),
        in_specs=[whole(pltpu.SMEM), whole(), whole(), whole()],
        out_specs=whole(pltpu.HBM),
        scratch_shapes=[
            pltpu.VMEM((SEQ * GROUPS, 2 * depth), jnp.float32),
            pltpu.VMEM((2 * depth, width), jnp.bfloat16),
            pltpu.VMEM((GROUPS, ROWS, width + HEAD), jnp.bfloat16),
            pltpu.SemaphoreType.DMA((GROUPS,)),
        ],
        compiler_params=pltpu.CompilerParams(vmem_limit_bytes=24 << 20),
        name="project",
    )(place, rows, w_own, w_other)


def rotate_kernel(parts, cos_ref, sin_ref, q_ref, kv_ref, held, sem):
    width = (HEADS + 2) * HEAD
    tail = sum(parts[g, :, width:].astype(jnp.float32) for g in range(GROUPS))
    squares = tail[:, :1] + tail[:, 1:2]
    inv = lax.rsqrt(squares / FEATURES + NORM_EPS)
    cosine, sine = cos_ref[...], sin_ref[...]
    sends = [pltpu.make_async_copy(held, kv_ref.at[m], sem.at[m]) for m in range(SAMP)]
    for h in (HEADS, HEADS + 1, *range(HEADS)):
        columns = pl.ds(h * HEAD, HEAD)
        u = sum(parts[g, :, columns].astype(jnp.float32) for g in range(GROUPS)) * inv
        if h <= HEADS:
            u = u * cosine + pltpu.roll(u, HEAD // 2, 1) * sine
        u = u.astype(jnp.bfloat16)
        if h < HEADS:
            q_ref[pl.ds(h * ROWS, ROWS), :] = u
        else:
            held[:, pl.ds((h - HEADS) * HEAD, HEAD)] = u
        if h == HEADS + 1:
            for send in sends:
                send.start()
    for send in sends:
        send.wait()


def rotate(parts, cosine, sine):
    return pl.pallas_call(
        rotate_kernel,
        out_shape=(
            jax.ShapeDtypeStruct((HEADS * ROWS, HEAD), jnp.bfloat16),
            pltpu.HBM((SAMP, ROWS, 2 * HEAD), jnp.bfloat16),
        ),
        in_specs=[whole()] * 3,
        out_specs=(whole(), whole(pltpu.HBM)),
        scratch_shapes=[
            pltpu.VMEM((ROWS, 2 * HEAD), jnp.bfloat16),
            pltpu.SemaphoreType.DMA((SAMP,)),
        ],
        compiler_params=pltpu.CompilerParams(vmem_limit_bytes=16 << 20),
        name="rotate",
    )(parts, cosine, sine)


def prefix_kernel(count, q_ref, kv_ref, acc_ref, max_ref, sum_ref, *, slots):
    step = pl.program_id(0)

    @pl.when(step == 0)
    def _():
        acc_ref[...] = jnp.zeros_like(acc_ref)
        max_ref[...] = jnp.full_like(max_ref, MASK_FILL)
        sum_ref[...] = jnp.zeros_like(sum_ref)

    first = step * slots

    def absorb(masked):
        keys, values = kv_ref[0, 0], kv_ref[1, 0]
        values = jnp.concatenate([values, jnp.ones_like(values)], axis=1)
        if masked:
            ids = first + lax.broadcasted_iota(jnp.int32, (1, slots), 1)
            bias = jnp.where(ids < count[0], 0.0, MASK_FILL)
        for h in range(HEADS):
            rows = pl.ds(h * ROWS, ROWS)
            scores = lax.dot_general(
                q_ref[rows, :], keys, LAST_DIMS, preferred_element_type=jnp.float32
            )
            if masked:
                scores = scores + bias
            old = max_ref[rows, :]
            new = jnp.maximum(old, jnp.max(scores, axis=1, keepdims=True))
            weights = jnp.exp2((scores - new[:, :1]) * LOG2_SCALE).astype(jnp.bfloat16)
            factor = jnp.exp2((old - new) * LOG2_SCALE)
            both = jnp.dot(weights, values, preferred_element_type=jnp.float32)
            acc_ref[rows, :] = acc_ref[rows, :] * factor + both[:, :HEAD]
            sum_ref[rows, :] = sum_ref[rows, :] * factor + both[:, HEAD:]
            max_ref[rows, :] = new

    @pl.when(first + slots <= count[0])
    def _():
        absorb(False)

    @pl.when((first < count[0]) & (first + slots > count[0]))
    def _():
        absorb(True)


def attend_prefix(count, queries, cache, slots=2048):
    n = queries.shape[0]
    state = jax.ShapeDtypeStruct((n, HEAD), jnp.float32)

    def cache_block(step, count):
        return (0, 0, jnp.minimum(step, lax.div(count[0] - 1, slots)), 0)

    return pl.pallas_call(
        functools.partial(prefix_kernel, slots=slots),
        out_shape=(state, state, state),
        grid_spec=pltpu.PrefetchScalarGridSpec(
            num_scalar_prefetch=1,
            grid=(cache.shape[2] // slots,),
            in_specs=[
                pl.BlockSpec((n, HEAD), lambda step, count: (0, 0)),
                pl.BlockSpec((2, 1, slots, HEAD), cache_block),
            ],
            out_specs=[pl.BlockSpec((n, HEAD), lambda step, count: (0, 0))] * 3,
        ),
        compiler_params=pltpu.CompilerParams(
            dimension_semantics=("arbitrary",), vmem_limit_bytes=24 << 20
        ),
        name="prefix",
    )(count, queries, cache)


def finish_kernel(place, q_ref, acc_ref, max_ref, sum_ref, kv, out, block, comp_block, sem):
    group, core = place[0], place[1]
    keys = jnp.concatenate([kv[m, :PROMPT_ROWS, :HEAD] for m in range(SAMP)], axis=0)
    values = jnp.concatenate([kv[m, :PROMPT_ROWS, HEAD:] for m in range(SAMP)], axis=0)
    values = jnp.concatenate([values, jnp.ones_like(values)], axis=1)
    first = 2 * (group - group % 2) + core
    comp = jnp.concatenate([kv[first, PROMPT_ROWS:, :], kv[first + 2, PROMPT_ROWS:, :]], axis=0)
    comp_values = jnp.concatenate([comp[:, HEAD:], jnp.ones_like(comp[:, HEAD:])], axis=1)
    n = keys.shape[0]
    column = lax.broadcasted_iota(jnp.int32, (1, n), 1)
    samp = column // PROMPT_ROWS
    key_id = 256 * (column // 16 % SEQ) + 128 * (samp % 2) + 16 * (samp // 2) + column % 16
    row = lax.broadcasted_iota(jnp.int32, (ROWS, 1), 0)
    own_id = 256 * (row // 16) + 128 * core + 16 * group + row % 16
    limit = jnp.where(row < PROMPT_ROWS, own_id, n)
    bias = jnp.where(key_id <= limit, 0.0, MASK_FILL)
    column = lax.broadcasted_iota(jnp.int32, (1, 2 * SEQ), 1)
    live = (column % SEQ == row - PROMPT_ROWS) & (column // SEQ <= group % 2)
    comp_bias = jnp.where(live, 0.0, MASK_FILL)
    for h in range(HEADS):
        rows = pl.ds(h * ROWS, ROWS)
        q = q_ref[rows, :]
        scores = lax.dot_general(q, keys, LAST_DIMS, preferred_element_type=jnp.float32) + bias
        comp_scores = (
            lax.dot_general(q, comp[:, :HEAD], LAST_DIMS, preferred_element_type=jnp.float32)
            + comp_bias
        )
        old = max_ref[rows, :]
        new = jnp.maximum(old, jnp.max(scores, axis=1, keepdims=True))
        new = jnp.maximum(new, jnp.max(comp_scores, axis=1, keepdims=True))
        weights = jnp.exp2((scores - new[:, :1]) * LOG2_SCALE).astype(jnp.bfloat16)
        comp_weights = jnp.exp2((comp_scores - new[:, :1]) * LOG2_SCALE).astype(jnp.bfloat16)
        factor = jnp.exp2((old - new) * LOG2_SCALE)
        both = jnp.dot(weights, values, preferred_element_type=jnp.float32)
        both = both + jnp.dot(comp_weights, comp_values, preferred_element_type=jnp.float32)
        context = acc_ref[rows, :] * factor + both[:, :HEAD]
        context = context / (sum_ref[rows, :] * factor + both[:, HEAD:])
        for s in range(SEQ):
            block[s, pl.ds(16 * h, 16), :] = context[16 * s : 16 * s + 16].astype(jnp.bfloat16)
            comp_block[s, pl.ds(h, 1), :] = context[PROMPT_ROWS + s : PROMPT_ROWS + s + 1]
    for s in range(SEQ):
        block[s, PROMPT_ROWS:, :] = comp_block[s].astype(jnp.bfloat16)

    def send(g):
        return pltpu.make_async_copy(block, out.at[:, g], sem.at[g])

    for g in range(GROUPS):
        send(g).start()
    for g in range(GROUPS):
        send(g).wait()


def finish(place, queries, state, kv):
    return pl.pallas_call(
        finish_kernel,
        out_shape=pltpu.HBM((SEQ, GROUPS, ROWS, HEAD), jnp.bfloat16),
        in_specs=[whole(pltpu.SMEM)] + [whole()] * 5,
        out_specs=whole(pltpu.HBM),
        scratch_shapes=[
            pltpu.VMEM((SEQ, ROWS, HEAD), jnp.bfloat16),
            pltpu.VMEM((SEQ, HEADS, HEAD), jnp.float32),
            pltpu.SemaphoreType.DMA((GROUPS,)),
        ],
        compiler_params=pltpu.CompilerParams(vmem_limit_bytes=28 << 20),
        name="finish",
    )(place, queries, *state, kv)


def output_kernel(place, source, kept, came, same, crossed, *refs):
    weights, (prompt_out, comp_out, matrix, sem) = refs[:SEQ], refs[SEQ:]
    loads = [pltpu.make_async_copy(w, matrix.at[j], sem.at[j]) for j, w in enumerate(weights)]
    for load in loads:
        load.start()
    core = place[1]
    blocks = (same, crossed)
    n = SAMP * HEADS
    to_row = lax.broadcasted_iota(jnp.int32, (n, n), 0)
    from_row = lax.broadcasted_iota(jnp.int32, (n, n), 1)
    head, out_row = to_row // SAMP, to_row % SAMP
    crossing = (out_row // GROUPS + core) % 2
    wanted = crossing * (GROUPS * HEADS) + (out_row % GROUPS) * HEADS + head
    order = jnp.where(from_row == wanted, 1.0, 0.0).astype(jnp.bfloat16)
    total = jnp.zeros((SAMP * 17, prompt_out.shape[1]), jnp.float32)
    for j in range(SEQ):
        first = source[j] * GROUPS
        left = []
        for b in blocks:
            for g in range(GROUPS):
                parts = [b[first + g, pl.ds(16 * h, 16), :] for h in range(HEADS)]
                left.append(jnp.concatenate(parts, axis=1))
        comp = [b[first + g, PROMPT_ROWS:, :] for b in blocks for g in range(GROUPS)]
        comp = jnp.concatenate(comp, axis=0)
        comp = jnp.dot(order, comp, preferred_element_type=jnp.float32).astype(jnp.bfloat16)
        parts = [comp[SAMP * h : SAMP * h + SAMP] for h in range(HEADS)]
        left.append(jnp.concatenate(parts, axis=1))
        left = jnp.concatenate(left, axis=0)
        loads[j].wait()
        total = total + jnp.dot(left, matrix[j], preferred_element_type=jnp.float32)
    rests = (kept, came)
    for r in range(2):
        at = pl.ds(pl.multiple_of(((core + r) % 2) * PROMPT_ROWS, PROMPT_ROWS), PROMPT_ROWS)
        rest = rests[r][:PROMPT_ROWS, :].astype(jnp.float32)
        prompt_out[at, :] = (total[PROMPT_ROWS * r : PROMPT_ROWS * (r + 1)] + rest).astype(
            jnp.bfloat16
        )
    low = jnp.concatenate([kept[PROMPT_ROWS:, :], came[PROMPT_ROWS:, :]], axis=0)
    high = jnp.concatenate([came[PROMPT_ROWS:, :], kept[PROMPT_ROWS:, :]], axis=0)
    rest = jnp.where(core == 0, low.astype(jnp.float32), high.astype(jnp.float32))
    comp_out[...] = (total[2 * PROMPT_ROWS :] + rest).astype(jnp.bfloat16)


def output(place, source, kept, came, same, crossed, weights):
    width = kept.shape[1]
    return pl.pallas_call(
        output_kernel,
        out_shape=(
            jax.ShapeDtypeStruct((2 * PROMPT_ROWS, width), jnp.bfloat16),
            jax.ShapeDtypeStruct((SAMP, width), jnp.bfloat16),
        ),
        in_specs=[whole(pltpu.SMEM)] * 2 + [whole()] * 4 + [whole(pl.ANY)] * SEQ,
        out_specs=(whole(), whole()),
        scratch_shapes=[
            pltpu.VMEM((SEQ, HEADS * HEAD, width), jnp.bfloat16),
            pltpu.SemaphoreType.DMA((SEQ,)),
        ],
        compiler_params=pltpu.CompilerParams(vmem_limit_bytes=30 << 20),
        name="output",
    )(place, source, kept, came, same, crossed, *weights)


def body(
    prompt_ids,
    comp_ids,
    prefix_len,
    prompt_offset,
    embed_table,
    attn_gain,
    query_key_value_weight,
    w_out,
    key_value_cache,
):
    seq_index = lax.axis_index("seq")
    samp_index = lax.axis_index("samp")
    group, core = samp_index // 2, samp_index % 2
    place = jnp.stack([group, core]).astype(jnp.int32)
    vocab_rows, width = embed_table.shape

    ids = [prompt_ids.reshape(SEQ, 2, PROMPT_ROWS), comp_ids.reshape(SEQ, 2, GROUPS)]
    ids = jnp.concatenate(ids, axis=2)
    local = jnp.clip(ids.reshape(-1) - seq_index * vocab_rows, 0, vocab_rows - 1)
    picked = embed_table.at[local].get(mode="promise_in_bounds").reshape(2 * SEQ, ROWS, width)
    got = exchange(picked, ("seq", "samp"), SEQ_CORE)
    own_ids = lax.dynamic_index_in_dim(ids.reshape(-1, ROWS), 2 * seq_index + core, 0, keepdims=False)
    copies, kept, given = merge(place, got, (own_ids // vocab_rows)[:, None])

    scaled = query_key_value_weight.astype(jnp.float32) * attn_gain.astype(jnp.float32)[:, None]
    scaled = scaled.astype(jnp.bfloat16)
    scaled_other = to_other_core(scaled)
    out_flip = to_seq(w_out, (0, 1))

    rows = exchange(copies, "seq")
    came = to_other_core(given)
    partial = project(place, rows, scaled, scaled_other)
    parts = exchange(partial, "samp", SAME_CORE)

    w_own, w_flip, _ = lax.optimization_barrier((w_out, out_flip, rows))
    w_next, w_last = to_seq(w_own, (3, 0)), to_seq(w_own, (1, 0))
    w_flip, w_next, w_last = lax.optimization_barrier((w_flip, w_next, w_last))
    w_next_flip, w_last_flip = to_seq(w_flip, (3, 0)), to_seq(w_flip, (1, 0))
    w_far = to_seq(w_next, (3, 0))

    row = jnp.arange(ROWS, dtype=jnp.int32)
    own_prompt = 256 * (row // 16) + 128 * core + 16 * group + row % 16
    position = jnp.where(row < PROMPT_ROWS, own_prompt, 2048 + group % 2) + prompt_offset[0]
    angles = position.astype(jnp.float32)[:, None] * rope_freqs(HEAD)[None, :]
    cosine, sine = jnp.cos(angles), jnp.sin(angles)
    cosine = jnp.concatenate([cosine, cosine], axis=1)
    sine = jnp.concatenate([-sine, sine], axis=1)
    queries, kv = rotate(parts, cosine, sine)
    all_kv = exchange(kv, "samp")
    queries, w_last_flip = lax.optimization_barrier((queries, w_last_flip))
    w_far_flip = to_seq(w_last_flip, (1, 0))
    state = attend_prefix(prefix_len, queries, key_value_cache)
    weights = [w_own, w_flip, w_next, w_next_flip, w_last, w_last_flip, w_far, w_far_flip]
    context = finish(place, queries, state, all_kv).reshape(SEQ * GROUPS, ROWS, HEAD)

    same = exchange(context, ("seq", "samp"), SEQ_GROUP)
    crossed = to_other_core(same)
    source = jnp.stack([moved(seq_index, shift) for shift in SHIFTS]).astype(jnp.int32)
    prompt_out, comp_out = output(place, source, kept, came, same, crossed, weights)
    return prompt_out, comp_out.reshape(8, 2, width)


def solution(mesh):
    placed = (
        P(),
        P(),
        P(),
        P(),
        P("seq", "samp"),
        P("samp"),
        P("samp", "seq"),
        P("seq", "samp"),
        P(None, "seq", None, None),
    )
    return jax.shard_map(
        body,
        mesh=mesh,
        in_specs=placed,
        out_specs=(P("seq", "samp"), P("seq", None, "samp")),
        check_vma=False,
    )
```

profile of v0, /device:TPU:6, one launch (start us, length us, event | category | flops | bytes accessed | tf_op | source)
XLA Modules:
  0.0 332.4 jit_solution(3770496859210589045)
XLA Ops:
  2.4 12.0 %gather_fusion = bf16[2176,512]{1,0:T(8,128)(2,1)} fusion(bf16[8016,512]{1,0:T(8,128)(2,1)} %param.13, s32[3072]{0:T(1024)S(1)} %pad_clamp_fusion), kind=kCustom, calls=%fused_computation | custom fusion | bytes 4465152 | tf_op jit(solution)/shard_map/gather | solution.py:421
  14.3 5.9 %all-to-all-start = ((bf16[16,136,512]{2,1,0:T(8,128)(2,1)}), bf16[16,136,512]{2,1,0:T(8,128)(2,1)S(1)}, u32[]{:S(2)}, u32[]{:S(2)}) async-start(bf16[16,136,512]{2,1,0:T(8,128)(2,1)} %bitcast.20), calls=%async_computation | async-start | bytes 4456448 | tf_op jit(solution)/shard_map/all_to_all | solution.py:56
  20.7 26.6 %all-to-all-done.got = bf16[16,136,512]{2,1,0:T(8,128)(2,1)S(1)} async-done(((bf16[16,136,512]{2,1,0:T(8,128)(2,1)}), bf16[16,136,512]{2,1,0:T(8,128)(2,1)S(1)}, u32[]{:S(2)}, u32[]{:S(2)}) %all-to-all-start) | async-done | bytes 2228256 | tf_op jit(solution)/shard_map/all_to_all | solution.py:56
  47.3 3.1 merge.1
  51.1 7.1 %all-to-all-start.1 = ((bf16[8,136,1024]{2,1,0:T(8,128)(2,1)}), bf16[8,136,1024]{2,1,0:T(8,128)(2,1)S(1)}, u32[]{:S(2)}, u32[]{:S(2)}) async-start(bf16[8,136,1024]{2,1,0:T(8,128)(2,1)} %get-tuple-element.21), calls=%async_computation.1 | async-start | bytes 4456448 | tf_op jit(solution)/shard_map/all_to_all | solution.py:56
  58.2 1.6 multiply_convert_fusion.w_own
  59.9 3.0 collective-permute-done.1.w_other
  64.0 25.5 %all-to-all-done.1.rows = bf16[8,136,1024]{2,1,0:T(8,128)(2,1)S(1)} async-done(((bf16[8,136,1024]{2,1,0:T(8,128)(2,1)}), bf16[8,136,1024]{2,1,0:T(8,128)(2,1)S(1)}, u32[]{:S(2)}, u32[]{:S(2)}) %all-to-all-start.1) | async-done | bytes 2228256 | tf_op jit(solution)/shard_map/all_to_all | solution.py:56
  90.8 6.2 %project.1 = bf16[8,136,1408]{2,1,0:T(8,128)(2,1)} custom-call(s32[2]{0:T(128)S(1)} %pad_add_fusion.place, bf16[8,136,1024]{2,1,0:T(8,128)(2,1)S(1)} %all-to-all-done.1.rows, bf16[512,1280]{1,0:T(8,128)(2,1)S(1)} %multiply_convert_fusion.w_own, bf16[512,1280]{1,0:T(8,128)(2,1)S(1)} %copy-done.2), custom_call_target="tpu_custom_call" | custom-call | tf_op jit(solution)/shard_map/project/pallas_call | solution.py:145
  97.0 7.7 %all-to-all-start.2 = ((bf16[8,136,1408]{2,1,0:T(8,128)(2,1)}), bf16[8,136,1408]{2,1,0:T(8,128)(2,1)S(1)}, u32[]{:S(2)}, u32[]{:S(2)}) async-start(bf16[8,136,1408]{2,1,0:T(8,128)(2,1)} %project.1), calls=%async_computation.2 | async-start | bytes 6127616 | tf_op jit(solution)/shard_map/all_to_all | solution.py:56
  104.6 54.8 %collective-permute-done.2.refs_1_ = bf16[1024,512]{1,0:T(8,128)(2,1)} collective-permute-done((bf16[1024,512]{1,0:T(8,128)(2,1)}, bf16[1024,512]{1,0:T(8,128)(2,1)}, u32[]{:S(2)}, u32[]{:S(2)}) %collective-permute-start.2) | collective-permute-done | bytes 1048608 | tf_op jit(solution)/shard_map/ppermute | solution.py:48
  159.4 3.2 collective-permute-start.4
  163.7 20.5 %collective-permute-done.3.refs_2_ = bf16[1024,512]{1,0:T(8,128)(2,1)} collective-permute-done((bf16[1024,512]{1,0:T(8,128)(2,1)}, bf16[1024,512]{1,0:T(8,128)(2,1)}, u32[]{:S(2)}, u32[]{:S(2)}) %collective-permute-start.3) | collective-permute-done | bytes 1048608 | tf_op jit(solution)/shard_map/ppermute | solution.py:48
  184.2 3.0 collective-permute-start.5
  188.7 6.8 %all-to-all-start.3 = ((bf16[16,136,256]{2,1,0:T(8,128)(2,1)}), bf16[16,136,256]{2,1,0:T(8,128)(2,1)S(1)}, u32[]{:S(2)}, u32[]{:S(2)}) async-start(bf16[16,136,256]{2,1,0:T(8,128)(2,1)} %get-tuple-element.30), calls=%async_computation.3 | async-start | bytes 2228224 | tf_op jit(solution)/shard_map/all_to_all | solution.py:56
  196.1 10.9 %collective-permute-done.5.refs_5_ = bf16[1024,512]{1,0:T(8,128)(2,1)} collective-permute-done((bf16[1024,512]{1,0:T(8,128)(2,1)}, bf16[1024,512]{1,0:T(8,128)(2,1)}, u32[]{:S(2)}, u32[]{:S(2)}) %collective-permute-start.5) | collective-permute-done | bytes 1048608 | tf_op jit(solution)/shard_map/ppermute | solution.py:48
  207.0 3.4 %copy-done = bf16[2,1,16384,128]{3,2,1,0:T(8,128)(2,1)S(1)} copy-done((bf16[2,1,16384,128]{3,2,1,0:T(8,128)(2,1)S(1)}, bf16[2,1,16384,128]{3,2,1,0:T(8,128)(2,1)}, u32[]{:S(2)}) %copy-start) | copy-done | bytes 8388632
  210.4 17.8 %prefix.1 = (f32[1088,128]{1,0:T(8,128)S(1)}, f32[1088,128]{1,0:T(8,128)S(1)}, f32[1088,128]{1,0:T(8,128)S(1)}) custom-call(s32[1]{0:T(128)S(6)} %copy.18.count, bf16[1088,128]{1,0:T(8,128)(2,1)S(1)} %get-tuple-element.26.q_ref, bf16[2,1,16384,128]{3,2,1,0:T(8,128)(2,1)S(1)} %copy-done), custom_call_target="tpu_custom_call" | custom-call | tf_op jit(solution)/shard_map/prefix/pallas_call | solution.py:252
  228.2 6.5 %finish.1 = bf16[8,8,136,128]{3,2,1,0:T(8,128)(2,1)} custom-call(s32[2]{0:T(128)S(1)} %pad_add_fusion.place, bf16[1088,128]{1,0:T(8,128)(2,1)S(1)} %get-tuple-element.26.q_ref, f32[1088,128]{1,0:T(8,128)S(1)} %get-tuple-element.27.acc_ref, f32[1088,128]{1,0:T(8,128)S(1)} %get-tuple-element.28.max_ref, f32[1088,128]{1,0:T(8,128)S(1)} %get-tuple-element.29.sum_ref, ...), custom_call_target="tpu_custom_call" | custom-call | tf_op jit(solution)/shard_map/finish/pallas_call | solution.py:324
  234.7 37.7 %all_to_all.25.same = bf16[64,136,128]{2,1,0:T(8,128)(2,1)S(1)} all-to-all(bf16[64,136,128]{2,1,0:T(8,128)(2,1)} %bitcast.21), channel_id=1, replica_groups={{0,2,4,6,8,10,12,14,16,18,20,22,24,26,28,30,32,34,36,38,40,42,44,46,48,..., dimensions={0} | all-to-all | bytes 4456448 | tf_op jit(solution)/shard_map/all_to_all | solution.py:56
  274.6 1.8 collective-permute-start.9
  278.0 22.0 %collective-permute-done.7.refs_3_ = bf16[1024,512]{1,0:T(8,128)(2,1)} collective-permute-done((bf16[1024,512]{1,0:T(8,128)(2,1)}, bf16[1024,512]{1,0:T(8,128)(2,1)}, u32[]{:S(2)}, u32[]{:S(2)}) %collective-permute-start.7) | collective-permute-done | bytes 1048608 | tf_op jit(solution)/shard_map/ppermute | solution.py:48
  299.9 22.0 %collective-permute-done.8.refs_6_ = bf16[1024,512]{1,0:T(8,128)(2,1)} collective-permute-done((bf16[1024,512]{1,0:T(8,128)(2,1)}, bf16[1024,512]{1,0:T(8,128)(2,1)}, u32[]{:S(2)}, u32[]{:S(2)}) %collective-permute-start.8) | collective-permute-done | bytes 1048608 | tf_op jit(solution)/shard_map/ppermute | solution.py:48
  323.2 7.2 %output.1 = (bf16[256,512]{1,0:T(8,128)(2,1)}, bf16[16,512]{1,0:T(8,128)(2,1)S(1)}) custom-call(s32[2]{0:T(128)S(1)} %copy-done.8, s32[8]{0:T(128)S(1)} %copy-done.9, bf16[136,512]{1,0:T(8,128)(2,1)S(1)} %copy-done.5, bf16[136,512]{1,0:T(8,128)(2,1)S(1)} %collective-permute-done.came, bf16[64,136,128]{2,1,0:T(8,128)(2,1)S(1)} %all_to_all.25.same, ...), custom_call_target="tpu_custom_call" | custom-call | tf_op jit(solution)/shard_map/output/pallas_call | solution.py:384
  (57 shorter events, 14.2 us)
Async XLA Ops:
  14.3 6.0 %copy-start.10 = (s32[2048]{0:T(1024)S(1)}, s32[2048]{0:T(1024)}, u32[]{:S(2)}) copy-start(s32[2048]{0:T(1024)} %param.9) | copy-start | bytes 24580
  14.3 33.0 %all-to-all-start = ((bf16[16,136,512]{2,1,0:T(8,128)(2,1)}), bf16[16,136,512]{2,1,0:T(8,128)(2,1)S(1)}, u32[]{:S(2)}, u32[]{:S(2)}) async-start(bf16[16,136,512]{2,1,0:T(8,128)(2,1)} %bitcast.20), calls=%async_computation | async-start | bytes 4456448 | tf_op jit(solution)/shard_map/all_to_all | solution.py:56
  20.7 207.5 %copy-start.7 = (s32[2]{0:T(128)}, s32[2]{0:T(128)S(1)}, u32[]{:S(2)}) copy-start(s32[2]{0:T(128)S(1)} %pad_add_fusion.place) | copy-start | bytes 28
  50.5 0.6 copy-start.4
  51.1 7.1 %copy-start.11 = (bf16[512]{0:T(512)(128)(2,1)S(1)}, bf16[512]{0:T(512)(128)(2,1)}, u32[]{:S(2)}) copy-start(bf16[512]{0:T(512)(128)(2,1)} %param.14) | copy-start | bytes 3076
  51.1 38.4 %all-to-all-start.1 = ((bf16[8,136,1024]{2,1,0:T(8,128)(2,1)}), bf16[8,136,1024]{2,1,0:T(8,128)(2,1)S(1)}, u32[]{:S(2)}, u32[]{:S(2)}) async-start(bf16[8,136,1024]{2,1,0:T(8,128)(2,1)} %get-tuple-element.21), calls=%async_computation.1 | async-start | bytes 4456448 | tf_op jit(solution)/shard_map/all_to_all | solution.py:56
  59.8 3.1 collective-permute-start.1
  62.9 1.1 copy-start.1
  89.5 1.3 copy-start.2
  97.0 90.3 %all-to-all-start.2 = ((bf16[8,136,1408]{2,1,0:T(8,128)(2,1)}), bf16[8,136,1408]{2,1,0:T(8,128)(2,1)S(1)}, u32[]{:S(2)}, u32[]{:S(2)}) async-start(bf16[8,136,1408]{2,1,0:T(8,128)(2,1)} %project.1), calls=%async_computation.2 | async-start | bytes 6127616 | tf_op jit(solution)/shard_map/all_to_all | solution.py:56
  104.6 54.8 %collective-permute-start.2 = (bf16[1024,512]{1,0:T(8,128)(2,1)}, bf16[1024,512]{1,0:T(8,128)(2,1)}, u32[]{:S(2)}, u32[]{:S(2)}) collective-permute-start(bf16[1024,512]{1,0:T(8,128)(2,1)} %refs_0_), channel_id=1, source_target_pairs={{0,64},{16,80},{32,96},{48,112},{64,0},{80,16},{96,32},{112,48},{1... | collective-permute-start | bytes 3145736 | tf_op jit(solution)/shard_map/ppermute | solution.py:48
  159.4 24.7 %collective-permute-start.3 = (bf16[1024,512]{1,0:T(8,128)(2,1)}, bf16[1024,512]{1,0:T(8,128)(2,1)}, u32[]{:S(2)}, u32[]{:S(2)}) collective-permute-start(bf16[1024,512]{1,0:T(8,128)(2,1)} %refs_0_), channel_id=1, source_target_pairs={{0,48},{16,0},{32,16},{48,32},{64,112},{80,64},{96,80},{112,96},{1... | collective-permute-start | bytes 3145736 | tf_op jit(solution)/shard_map/ppermute | solution.py:48
  159.4 24.7 %collective-permute-start.4 = (bf16[1024,512]{1,0:T(8,128)(2,1)}, bf16[1024,512]{1,0:T(8,128)(2,1)}, u32[]{:S(2)}, u32[]{:S(2)}) collective-permute-start(bf16[1024,512]{1,0:T(8,128)(2,1)} %refs_0_), channel_id=1, source_target_pairs={{0,16},{16,32},{32,48},{48,0},{64,80},{80,96},{96,112},{112,64},{1... | collective-permute-start | bytes 3145736 | tf_op jit(solution)/shard_map/ppermute | solution.py:48
  184.2 22.9 %collective-permute-start.5 = (bf16[1024,512]{1,0:T(8,128)(2,1)}, bf16[1024,512]{1,0:T(8,128)(2,1)}, u32[]{:S(2)}, u32[]{:S(2)}) collective-permute-start(bf16[1024,512]{1,0:T(8,128)(2,1)} %collective-permute-done.2.refs_1_), channel_id=1, source_target_pairs={{0,16},{16,32},{32,48},{48,0},{64,80},{80,96},{96,112},{112,64},{1... | collective-permute-start | bytes 3145736 | tf_op jit(solution)/shard_map/ppermute | solution.py:48
  188.7 39.5 %all-to-all-start.3 = ((bf16[16,136,256]{2,1,0:T(8,128)(2,1)}), bf16[16,136,256]{2,1,0:T(8,128)(2,1)S(1)}, u32[]{:S(2)}, u32[]{:S(2)}) async-start(bf16[16,136,256]{2,1,0:T(8,128)(2,1)} %get-tuple-element.30), calls=%async_computation.3 | async-start | bytes 2228224 | tf_op jit(solution)/shard_map/all_to_all | solution.py:56
  207.0 3.4 %copy-start = (bf16[2,1,16384,128]{3,2,1,0:T(8,128)(2,1)S(1)}, bf16[2,1,16384,128]{3,2,1,0:T(8,128)(2,1)}, u32[]{:S(2)}) copy-start(bf16[2,1,16384,128]{3,2,1,0:T(8,128)(2,1)} %kv_ref.1) | copy-start | bytes 25165828
  234.7 87.3 %copy-start.3 = (bf16[1024,512]{1,0:T(8,128)(2,1)S(1)}, bf16[1024,512]{1,0:T(8,128)(2,1)}, u32[]{:S(2)}) copy-start(bf16[1024,512]{1,0:T(8,128)(2,1)} %refs_0_) | copy-start | bytes 3145732
  234.7 87.3 %copy-start.5 = (bf16[136,512]{1,0:T(8,128)(2,1)S(1)}, bf16[136,512]{1,0:T(8,128)(2,1)}, u32[]{:S(2)}) copy-start(bf16[136,512]{1,0:T(8,128)(2,1)} %copy-done.4) | copy-start | bytes 417796
  272.4 49.6 %collective-permute-start.6 = (bf16[64,136,128]{2,1,0:T(8,128)(2,1)S(1)}, bf16[64,136,128]{2,1,0:T(8,128)(2,1)}, u32[]{:S(2)}, u32[]{:S(2)}) collective-permute-start(bf16[64,136,128]{2,1,0:T(8,128)(2,1)S(1)} %all_to_all.25.same), channel_id=1, source_target_pairs={{0,1},{1,0},{2,3},{3,2},{4,5},{5,4},{6,7},{7,6},{8,9},{9,8},{10,11... | collective-permute-start | bytes 6684680 | tf_op jit(solution)/shard_map/ppermute | solution.py:52
  272.4 27.6 %collective-permute-start.7 = (bf16[1024,512]{1,0:T(8,128)(2,1)}, bf16[1024,512]{1,0:T(8,128)(2,1)}, u32[]{:S(2)}, u32[]{:S(2)}) collective-permute-start(bf16[1024,512]{1,0:T(8,128)(2,1)} %collective-permute-done.2.refs_1_), channel_id=1, source_target_pairs={{0,48},{16,0},{32,16},{48,32},{64,112},{80,64},{96,80},{112,96},{1... | collective-permute-start | bytes 3145736 | tf_op jit(solution)/shard_map/ppermute | solution.py:48
  273.2 48.8 %collective-permute-start.8 = (bf16[1024,512]{1,0:T(8,128)(2,1)}, bf16[1024,512]{1,0:T(8,128)(2,1)}, u32[]{:S(2)}, u32[]{:S(2)}) collective-permute-start(bf16[1024,512]{1,0:T(8,128)(2,1)} %collective-permute-done.3.refs_2_), channel_id=1, source_target_pairs={{0,48},{16,0},{32,16},{48,32},{64,112},{80,64},{96,80},{112,96},{1... | collective-permute-start | bytes 3145736 | tf_op jit(solution)/shard_map/ppermute | solution.py:48
  274.6 47.4 %collective-permute-start.9 = (bf16[1024,512]{1,0:T(8,128)(2,1)}, bf16[1024,512]{1,0:T(8,128)(2,1)}, u32[]{:S(2)}, u32[]{:S(2)}) collective-permute-start(bf16[1024,512]{1,0:T(8,128)(2,1)} %collective-permute-done.5.refs_5_), channel_id=1, source_target_pairs={{0,16},{16,32},{32,48},{48,0},{64,80},{80,96},{96,112},{112,64},{1... | collective-permute-start | bytes 3145736 | tf_op jit(solution)/shard_map/ppermute | solution.py:48
  276.4 1.6 collective-permute-start
  322.0 0.6 copy-start.8
  (2 other events, 1.2 us)
where the time goes:
time: 334 us; the launch traced here: 332 us
  waiting for transfers between devices  186 us (56%)
  Pallas kernels  42.2 us (13%)
  starting transfers between devices  37.8 us (11%)
  blocking collectives  37.7 us (11%)
  local copies, waits for them, and re-layouts  23.4 us (7%)
    ppermute x7, waiting for transfers between devices, to_seq(): lax.ppermute(block, 'seq', [(i, moved(i, shift)) for i in range(SEQ)])  130 us
    all_to_all x4, waiting for transfers between devices, exchange(): lax.all_to_all(blocks, axes, 0, 0, tiled=True, axis_index_groups=groups)  52.1 us
    all_to_all x1, blocking collectives, exchange(): lax.all_to_all(blocks, axes, 0, 0, tiled=True, axis_index_groups=groups)  37.7 us
    all_to_all x4, starting transfers between devices, exchange(): lax.all_to_all(blocks, axes, 0, 0, tiled=True, axis_index_groups=groups)  27.5 us
    pallas_call x1, Pallas kernels, attend_prefix(): pl.pallas_call(functools.partial(prefix_kernel, slots=slots), out_shape=(...  17.8 us
    gather x1, local copies, waits for them, and re-layouts, body(): embed_table.at[local].get(mode='promise_in_bounds')  12 us
    ppermute x7, starting transfers between devices, to_seq(): lax.ppermute(block, 'seq', [(i, moved(i, shift)) for i in range(SEQ)])  10.2 us
    unnamed x25, local copies, waits for them, and re-layouts  9.02 us
  transfers between devices with their start and end apart: 14, of which 9 were waited for; matrix products, arithmetic and copies ran while one was open for 1% of the time, Pallas kernels for 6%

commit v1 on v0

v1 whole, which is shorter than its diff:
```python
import functools
import math

import jax
import jax.numpy as jnp
from jax import lax
from jax.experimental import pallas as pl
from jax.experimental.pallas import tpu as pltpu
from jax.sharding import PartitionSpec as P


NORM_EPS = 1e-05
MASK_FILL = -1e30
HEAD = 128
HEADS = 8
SEQ = 8
GROUPS = 8
SAMP = 16
ROWS = 136
PROMPT_ROWS = 128
FEATURES = 8192
LOG2_SCALE = math.log2(math.e) / math.sqrt(HEAD)
LAST_DIMS = (((1,), (1,)), ((), ()))

SLOTS = 8
TILES = 4
SEQ_SLOT = [[SAMP * s + 8 * pair + f for s in range(SEQ) for f in range(SLOTS)] for pair in range(2)]
SAME_PAIR = [[8 * pair + f for f in range(SLOTS)] for pair in range(2)]
SEQ_GROUP = [[SAMP * s + 2 * g + c for s in range(SEQ) for g in range(GROUPS)] for c in range(2)]
SHIFTS = ((0, 0), (0, 1), (1, 0), (1, 1), (3, 0), (3, 1), (2, 0), (2, 1))


def rope_freqs(head_dim):
    half_dim = head_dim // 2
    dim_index = jnp.arange(half_dim, dtype=jnp.float32)
    base_freq = 1.0 / jnp.power(500000.0, 2.0 * dim_index / head_dim)
    wavelength = 2.0 * math.pi / base_freq
    blend = (8192.0 / wavelength - 1.0) / 3.0
    middle = (1.0 - blend) * base_freq / 8.0 + blend * base_freq
    return jnp.where(
        wavelength > 8192.0, base_freq / 8.0, jnp.where(wavelength < 2048.0, base_freq, middle)
    )


def moved(index, shift, sign=1):
    return (index % 4 + sign * shift[0] + 4) % 4 + 4 * ((index // 4) ^ shift[1])


def to_seq(block, shift):
    return lax.ppermute(block, "seq", [(i, moved(i, shift)) for i in range(SEQ)])


def to_other_core(block):
    return lax.ppermute(block, "samp", [(i, i ^ 1) for i in range(SAMP)])


def to_ring(block, step):
    pairs = [(m, m // 8 * 8 + (m % 8 + 2 * step) % 8) for m in range(SAMP)]
    return lax.ppermute(block, "samp", pairs)


def to_other_pair(block):
    return lax.ppermute(block, "samp", [(m, (m + 8) % SAMP) for m in range(SAMP)])


def exchange(blocks, axes, groups=None):
    return lax.all_to_all(blocks, axes, 0, 0, tiled=True, axis_index_groups=groups)


def whole(memory_space=pltpu.VMEM):
    return pl.BlockSpec(memory_space=memory_space)


def selection(rows, columns, wanted):
    row = lax.broadcasted_iota(jnp.int32, (rows, columns), 0)
    column = lax.broadcasted_iota(jnp.int32, (rows, columns), 1)
    return jnp.where(column == wanted(row), 1.0, 0.0).astype(jnp.bfloat16)


def selected(matrix, block):
    return jnp.dot(matrix, block, preferred_element_type=jnp.float32)


def arrange_kernel(picked, out, comp, sem):
    n = SEQ * SLOTS
    sends = [
        pltpu.make_async_copy(
            picked.at[pl.ds(0, n), :, pl.ds(HEAD * k, HEAD)], out.at[:, pl.ds(32 * k, 32), :], sem.at[k]
        )
        for k in range(TILES)
    ]
    for send in sends:
        send.start()
    rows = jnp.concatenate([picked[n + i] for i in range(4)], axis=0)
    total = jnp.zeros((8 * n, HEAD), jnp.float32)
    for k in range(TILES):
        matrix = selection(
            8 * n, 2 * n, lambda r: jnp.where(r // 2 % TILES == k, r // 8 * 2 + r % 2, -1)
        )
        total = total + selected(matrix, rows[:, HEAD * k : HEAD * k + HEAD])
    comp[...] = total.astype(jnp.bfloat16).reshape(n, 8, HEAD)
    last = pltpu.make_async_copy(comp, out.at[:, pl.ds(PROMPT_ROWS, 8), :], sem.at[TILES])
    last.start()
    for send in sends + [last]:
        send.wait()


def arrange(picked):
    n = SEQ * SLOTS
    return pl.pallas_call(
        arrange_kernel,
        out_shape=pltpu.HBM((n, ROWS, HEAD), jnp.bfloat16),
        in_specs=[whole()],
        out_specs=whole(pltpu.HBM),
        scratch_shapes=[
            pltpu.VMEM((n, 8, HEAD), jnp.bfloat16),
            pltpu.SemaphoreType.DMA((TILES + 1,)),
        ],
        compiler_params=pltpu.CompilerParams(vmem_limit_bytes=16 << 20),
        name="arrange",
    )(picked)


def merge_kernel(got, owner, copies, merged, held, sem):
    sends = [pltpu.make_async_copy(held, copies.at[s], sem.at[s]) for s in range(SEQ)]
    sends.append(pltpu.make_async_copy(held, merged, sem.at[SEQ]))
    owns = [owner[...] == s for s in range(SEQ)]
    for f in range(SLOTS):
        total = jnp.zeros((ROWS, HEAD), jnp.float32)
        for s in range(SEQ):
            total = jnp.where(owns[s], got[SLOTS * s + f].astype(jnp.float32), total)
        held[f] = total.astype(jnp.bfloat16)
    for send in sends:
        send.start()
    for send in sends:
        send.wait()


def merge(got, owner):
    return pl.pallas_call(
        merge_kernel,
        out_shape=(
            pltpu.HBM((SEQ, SLOTS, ROWS, HEAD), jnp.bfloat16),
            pltpu.HBM((SLOTS, ROWS, HEAD), jnp.bfloat16),
        ),
        in_specs=[whole(), whole()],
        out_specs=(whole(pltpu.HBM), whole(pltpu.HBM)),
        scratch_shapes=[
            pltpu.VMEM((SLOTS, ROWS, HEAD), jnp.bfloat16),
            pltpu.SemaphoreType.DMA((SEQ + 1,)),
        ],
        compiler_params=pltpu.CompilerParams(vmem_limit_bytes=16 << 20),
        name="merge",
    )(got, owner)


def project_kernel(rows, *refs):
    weights, (kept, sent, matrix, total, own, other, sem) = refs[:SLOTS], refs[SLOTS:]
    loads = [pltpu.make_async_copy(w, matrix.at[j], sem.at[j]) for j, w in enumerate(weights)]
    for load in loads:
        load.start()
    samp = lax.axis_index("samp")
    pair, slot = samp // 8, samp % 8
    slots = [(slot // 2 + step) % 4 * 2 + (slot + cross) % 2 for cross in (0, 1) for step in (0, 1, 3, 2)]
    n = 8 * SEQ
    orders = [
        selection(
            2 * SEQ, n, lambda r: r % SEQ * 8 + 2 * k + jnp.where(pair == 0, r // SEQ, 1 - r // SEQ)
        )
        for k in range(TILES)
    ]
    squares = jnp.zeros((2 * ROWS, 1), jnp.float32)
    for j in range(SLOTS):
        f = slots[j]
        comp = jnp.concatenate([rows[s, f, PROMPT_ROWS:, :] for s in range(SEQ)], axis=0)
        comp = [selected(order, comp).astype(jnp.bfloat16) for order in orders]
        comp = jnp.concatenate(comp, axis=1)
        parts = []
        for r in range(2):
            first = 16 * ((pair + r) % 2)
            for s in range(SEQ):
                tiles = [
                    rows[s, f, pl.ds(pl.multiple_of(32 * k + first, 16), 16), :] for k in range(TILES)
                ]
                parts.append(jnp.concatenate(tiles, axis=1))
            parts.append(comp[SEQ * r : SEQ * r + SEQ])
        block = jnp.concatenate(parts, axis=0)
        wide = block.astype(jnp.float32)
        squares = squares + jnp.sum(wide * wide, axis=1, keepdims=True)
        loads[j].wait()
        product = jnp.dot(block, matrix[j], preferred_element_type=jnp.float32)
        if j == 0:
            total[...] = product
        elif j < SLOTS - 1:
            total[...] += product
        else:
            product = total[...] + product
    high = squares.astype(jnp.bfloat16).astype(jnp.float32)
    lane = lax.broadcasted_iota(jnp.int32, (2 * ROWS, HEAD), 1)
    extra = jnp.where(lane == 0, high, jnp.where(lane == 1, squares - high, 0.0))
    width = product.shape[1]
    for r, out in enumerate((own, other)):
        out[:, :width] = product[ROWS * r : ROWS * r + ROWS].astype(jnp.bfloat16)
        out[:, width:] = extra[ROWS * r : ROWS * r + ROWS].astype(jnp.bfloat16)
    sends = [
        pltpu.make_async_copy(other, sent, sem.at[SLOTS]),
        pltpu.make_async_copy(own, kept, sem.at[SLOTS + 1]),
    ]
    for send in sends:
        send.start()
    for send in sends:
        send.wait()


def project(rows, weights):
    depth, width = weights[0].shape
    shape = (ROWS, width + HEAD)
    return pl.pallas_call(
        project_kernel,
        out_shape=(pltpu.HBM(shape, jnp.bfloat16), pltpu.HBM(shape, jnp.bfloat16)),
        in_specs=[whole()] + [whole(pl.ANY)] * SLOTS,
        out_specs=(whole(pltpu.HBM), whole(pltpu.HBM)),
        scratch_shapes=[
            pltpu.VMEM((SLOTS, depth, width), jnp.bfloat16),
            pltpu.VMEM((2 * ROWS, width), jnp.float32),
            pltpu.VMEM(shape, jnp.bfloat16),
            pltpu.VMEM(shape, jnp.bfloat16),
            pltpu.SemaphoreType.DMA((SLOTS + 2,)),
        ],
        compiler_params=pltpu.CompilerParams(vmem_limit_bytes=28 << 20),
        name="project",
    )(rows, *weights)


def rotate_kernel(kept, given, cos_ref, sin_ref, q_ref, kv_ref, held, mine, sem):
    load = pltpu.make_async_copy(kept, mine, sem.at[SAMP])
    load.start()
    load.wait()
    width = (HEADS + 2) * HEAD
    tail = sum(p[:, width:].astype(jnp.float32) for p in (mine, given))
    squares = tail[:, :1] + tail[:, 1:2]
    inv = lax.rsqrt(squares / FEATURES + NORM_EPS)
    cosine, sine = cos_ref[...], sin_ref[...]
    sends = [pltpu.make_async_copy(held, kv_ref.at[m], sem.at[m]) for m in range(SAMP)]
    for h in (HEADS, HEADS + 1, *range(HEADS)):
        columns = pl.ds(h * HEAD, HEAD)
        u = sum(p[:, columns].astype(jnp.float32) for p in (mine, given)) * inv
        if h <= HEADS:
            u = u * cosine + pltpu.roll(u, HEAD // 2, 1) * sine
        if h < HEADS:
            u = u * LOG2_SCALE
        u = u.astype(jnp.bfloat16)
        if h < HEADS:
            q_ref[pl.ds(h * ROWS, ROWS), :] = u
        else:
            held[:, pl.ds((h - HEADS) * HEAD, HEAD)] = u
        if h == HEADS + 1:
            for send in sends:
                send.start()
    for send in sends:
        send.wait()


def rotate(mine, given, cosine, sine):
    return pl.pallas_call(
        rotate_kernel,
        out_shape=(
            jax.ShapeDtypeStruct((HEADS * ROWS, HEAD), jnp.bfloat16),
            pltpu.HBM((SAMP, ROWS, 2 * HEAD), jnp.bfloat16),
        ),
        in_specs=[whole(pl.ANY)] + [whole()] * 3,
        out_specs=(whole(), whole(pltpu.HBM)),
        scratch_shapes=[
            pltpu.VMEM((ROWS, 2 * HEAD), jnp.bfloat16),
            pltpu.VMEM(mine.shape, jnp.bfloat16),
            pltpu.SemaphoreType.DMA((SAMP + 1,)),
        ],
        compiler_params=pltpu.CompilerParams(vmem_limit_bytes=16 << 20),
        name="rotate",
    )(mine, given, cosine, sine)


def prefix_kernel(count, q_ref, kv_ref, acc_ref, max_ref, sum_ref, token_ref, *, slots):
    step = pl.program_id(0)

    @pl.when(step == 0)
    def _():
        acc_ref[...] = jnp.zeros_like(acc_ref)
        max_ref[...] = jnp.full_like(max_ref, MASK_FILL)
        sum_ref[...] = jnp.zeros_like(sum_ref)
        token_ref[...] = jnp.zeros_like(token_ref)

    first = step * slots

    def absorb(masked):
        keys, values = kv_ref[0, 0], kv_ref[1, 0]
        values = jnp.concatenate([values, jnp.ones_like(values)], axis=1)
        if masked:
            ids = first + lax.broadcasted_iota(jnp.int32, (1, slots), 1)
            bias = jnp.where(ids < count[0], 0.0, MASK_FILL)
        for h in range(HEADS):
            rows = pl.ds(h * ROWS, ROWS)
            scores = lax.dot_general(
                q_ref[rows, :], keys, LAST_DIMS, preferred_element_type=jnp.float32
            )
            if masked:
                scores = scores + bias
            old = max_ref[rows, :]
            new = jnp.maximum(old, jnp.max(scores, axis=1, keepdims=True))
            weights = jnp.exp2(scores - new[:, :1]).astype(jnp.bfloat16)
            factor = jnp.exp2(old - new)
            both = jnp.dot(weights, values, preferred_element_type=jnp.float32)
            acc_ref[rows, :] = acc_ref[rows, :] * factor + both[:, :HEAD]
            sum_ref[rows, :] = sum_ref[rows, :] * factor + both[:, HEAD:]
            max_ref[rows, :] = new

    @pl.when(first + slots <= count[0])
    def _():
        absorb(False)

    @pl.when((first < count[0]) & (first + slots > count[0]))
    def _():
        absorb(True)


def attend_prefix(count, queries, cache, slots=2048):
    n = queries.shape[0]
    state = jax.ShapeDtypeStruct((n, HEAD), jnp.float32)

    def cache_block(step, count):
        return (0, 0, jnp.minimum(step, lax.div(count[0] - 1, slots)), 0)

    return pl.pallas_call(
        functools.partial(prefix_kernel, slots=slots),
        out_shape=(state, state, state, jax.ShapeDtypeStruct((8, HEAD), jnp.float32)),
        grid_spec=pltpu.PrefetchScalarGridSpec(
            num_scalar_prefetch=1,
            grid=(cache.shape[2] // slots,),
            in_specs=[
                pl.BlockSpec((n, HEAD), lambda step, count: (0, 0)),
                pl.BlockSpec((2, 1, slots, HEAD), cache_block),
            ],
            out_specs=[pl.BlockSpec((n, HEAD), lambda step, count: (0, 0))] * 3
            + [pl.BlockSpec((8, HEAD), lambda step, count: (0, 0))],
        ),
        compiler_params=pltpu.CompilerParams(
            dimension_semantics=("arbitrary",), vmem_limit_bytes=14 << 20
        ),
        name="prefix",
    )(count, queries, cache)


def finish_kernel(q_ref, acc_ref, max_ref, sum_ref, kv, out, block, comp_block, sem):
    samp_index = lax.axis_index("samp")
    pair, slot = samp_index // 8, samp_index % 8
    keys = jnp.concatenate([kv[m, :PROMPT_ROWS, :HEAD] for m in range(SAMP)], axis=0)
    values = jnp.concatenate([kv[m, :PROMPT_ROWS, HEAD:] for m in range(SAMP)], axis=0)
    values = jnp.concatenate([values, jnp.ones_like(values)], axis=1)
    comp = jnp.concatenate([kv[slot + 8 * r, PROMPT_ROWS:, :] for r in range(2)], axis=0)
    comp_values = jnp.concatenate([comp[:, HEAD:], jnp.ones_like(comp[:, HEAD:])], axis=1)
    n = keys.shape[0]
    column = lax.broadcasted_iota(jnp.int32, (1, n), 1)
    samp = column // PROMPT_ROWS
    key_id = 256 * (column // 16 % SEQ) + 32 * (samp % 8) + 16 * (samp // 8) + column % 16
    row = lax.broadcasted_iota(jnp.int32, (ROWS, 1), 0)
    own_id = 256 * (row // 16) + 32 * slot + 16 * pair + row % 16
    limit = jnp.where(row < PROMPT_ROWS, own_id, n)
    bias = jnp.where(key_id <= limit, 0.0, MASK_FILL)
    column = lax.broadcasted_iota(jnp.int32, (1, 2 * SEQ), 1)
    live = (column % SEQ == row - PROMPT_ROWS) & (column // SEQ <= pair)
    comp_bias = jnp.where(live, 0.0, MASK_FILL)
    for h in range(HEADS):
        rows = pl.ds(h * ROWS, ROWS)
        q = q_ref[rows, :]
        scores = lax.dot_general(q, keys, LAST_DIMS, preferred_element_type=jnp.float32) + bias
        comp_scores = (
            lax.dot_general(q, comp[:, :HEAD], LAST_DIMS, preferred_element_type=jnp.float32)
            + comp_bias
        )
        old = max_ref[rows, :]
        new = jnp.maximum(old, jnp.max(scores, axis=1, keepdims=True))
        new = jnp.maximum(new, jnp.max(comp_scores, axis=1, keepdims=True))
        weights = jnp.exp2(scores - new[:, :1]).astype(jnp.bfloat16)
        comp_weights = jnp.exp2(comp_scores - new[:, :1]).astype(jnp.bfloat16)
        factor = jnp.exp2(old - new)
        both = jnp.dot(weights, values, preferred_element_type=jnp.float32)
        both = both + jnp.dot(comp_weights, comp_values, preferred_element_type=jnp.float32)
        context = acc_ref[rows, :] * factor + both[:, :HEAD]
        context = context / (sum_ref[rows, :] * factor + both[:, HEAD:])
        for s in range(SEQ):
            block[s, pl.ds(16 * h, 16), :] = context[16 * s : 16 * s + 16].astype(jnp.bfloat16)
            comp_block[s, pl.ds(h, 1), :] = context[PROMPT_ROWS + s : PROMPT_ROWS + s + 1]
    for s in range(SEQ):
        block[s, PROMPT_ROWS:, :] = comp_block[s].astype(jnp.bfloat16)

    def send(g):
        return pltpu.make_async_copy(block, out.at[:, g], sem.at[g])

    for g in range(GROUPS):
        send(g).start()
    for g in range(GROUPS):
        send(g).wait()


def finish(queries, state, kv):
    return pl.pallas_call(
        finish_kernel,
        out_shape=pltpu.HBM((SEQ, GROUPS, ROWS, HEAD), jnp.bfloat16),
        in_specs=[whole()] * 5,
        out_specs=whole(pltpu.HBM),
        scratch_shapes=[
            pltpu.VMEM((SEQ, ROWS, HEAD), jnp.bfloat16),
            pltpu.VMEM((SEQ, HEADS, HEAD), jnp.float32),
            pltpu.SemaphoreType.DMA((GROUPS,)),
        ],
        compiler_params=pltpu.CompilerParams(vmem_limit_bytes=14 << 20),
        name="finish",
    )(queries, *state, kv)


def output_kernel(rest, same, crossed, *refs):
    weights, (prompt_out, comp_out, matrix, sem) = refs[:SEQ], refs[SEQ:]
    loads = [pltpu.make_async_copy(w, matrix.at[j], sem.at[j]) for j, w in enumerate(weights)]
    for load in loads:
        load.start()
    core = lax.axis_index("samp") % 2
    seq = lax.axis_index("seq")
    blocks = (same, crossed)
    n = SAMP * HEADS

    def comp_source(r):
        head, token = r // SAMP, r % SAMP
        group = token % 2 * 4 + token // 4
        crossing = (token // 2 + core) % 2
        return (crossing * GROUPS + group) * HEADS + head

    order = selection(n, n, comp_source)
    total = jnp.zeros((SAMP * 17, matrix.shape[2]), jnp.float32)
    for j in range(SEQ):
        first = moved(seq, SHIFTS[j]) * GROUPS
        left = []
        for b in blocks:
            for g in range(GROUPS):
                parts = [b[first + g, pl.ds(16 * h, 16), :] for h in range(HEADS)]
                left.append(jnp.concatenate(parts, axis=1))
        comp = [b[first + g, PROMPT_ROWS:, :] for b in blocks for g in range(GROUPS)]
        comp = selected(order, jnp.concatenate(comp, axis=0)).astype(jnp.bfloat16)
        parts = [comp[SAMP * h : SAMP * h + SAMP] for h in range(HEADS)]
        left.append(jnp.concatenate(parts, axis=1))
        left = jnp.concatenate(left, axis=0)
        loads[j].wait()
        total = total + jnp.dot(left, matrix[j], preferred_element_type=jnp.float32)
    for r in range(2):
        for g in range(GROUPS):
            slot = 2 * (g % 4) + (core + r) % 2
            at = pl.multiple_of(32 * slot + 16 * (g // 4), 16)
            parts = [
                rest[slot, pl.ds(32 * k + 16 * (g // 4), 16), :].astype(jnp.float32)
                for k in range(TILES)
            ]
            i = 16 * (GROUPS * r + g)
            prompt_out[pl.ds(at, 16), :] = (
                total[i : i + 16] + jnp.concatenate(parts, axis=1)
            ).astype(jnp.bfloat16)
    comp = jnp.concatenate([rest[f, PROMPT_ROWS:, :] for f in range(SLOTS)], axis=0)
    parts = [
        selected(selection(SAMP, 8 * SLOTS, lambda r: r // 2 * 8 + 2 * k + r % 2), comp)
        for k in range(TILES)
    ]
    last = (total[2 * PROMPT_ROWS :] + jnp.concatenate(parts, axis=1)).astype(jnp.bfloat16)
    comp_out[...] = last.reshape(comp_out.shape)


def output(rest, same, crossed, weights):
    width = weights[0].shape[1]
    return pl.pallas_call(
        output_kernel,
        out_shape=(
            jax.ShapeDtypeStruct((2 * PROMPT_ROWS, width), jnp.bfloat16),
            jax.ShapeDtypeStruct((SAMP // 2, 2, width), jnp.bfloat16),
        ),
        in_specs=[whole()] * 3 + [whole(pl.ANY)] * SEQ,
        out_specs=(whole(), whole()),
        scratch_shapes=[
            pltpu.VMEM((SEQ, HEADS * HEAD, width), jnp.bfloat16),
            pltpu.SemaphoreType.DMA((SEQ,)),
        ],
        compiler_params=pltpu.CompilerParams(vmem_limit_bytes=30 << 20),
        name="output",
    )(rest, same, crossed, *weights)


def body(
    prompt_ids,
    comp_ids,
    prefix_len,
    prompt_offset,
    embed_table,
    attn_gain,
    query_key_value_weight,
    w_out,
    key_value_cache,
):
    seq_index = lax.axis_index("seq")
    samp_index = lax.axis_index("samp")
    pair, slot = samp_index // 8, samp_index % 8
    vocab_rows, width = embed_table.shape

    scaled = query_key_value_weight.astype(jnp.float32) * attn_gain.astype(jnp.float32)[:, None]
    scaled = scaled.astype(jnp.bfloat16)
    out_flip = to_seq(w_out, (0, 1))
    w_next, w_last = to_seq(w_out, (3, 0)), to_seq(w_out, (1, 0))
    scaled_next, scaled_last = to_ring(scaled, 3), to_ring(scaled, 1)

    ids = jnp.concatenate([prompt_ids, comp_ids.reshape(-1)])
    local = jnp.clip(ids - seq_index * vocab_rows, 0, vocab_rows - 1)
    picked = embed_table.at[local].get(mode="promise_in_bounds")
    pieces = arrange(picked.reshape(-1, 32, width))
    got = exchange(pieces, ("seq", "samp"), SEQ_SLOT)
    piece_at = SLOTS * seq_index + slot
    own_prompt_ids = lax.dynamic_slice_in_dim(prompt_ids, 32 * piece_at, 32, 0)
    own_comp_ids = lax.dynamic_slice_in_dim(comp_ids.reshape(-1), 2 * piece_at, 2, 0)
    own_ids = jnp.concatenate([jnp.tile(own_prompt_ids, TILES), jnp.tile(own_comp_ids, TILES)])
    owner = (own_ids // vocab_rows)[:, None]
    copies, merged = merge(got, owner)

    rows = exchange(copies, "seq")
    by_ring, _ = lax.optimization_barrier((scaled, copies))
    scaled_far = to_ring(by_ring, 2)
    scales = [scaled, scaled_next, scaled_last, scaled_far]
    scales = scales + [to_other_core(w) for w in scales]
    mine, sent = project(rows, scales)
    given = to_other_pair(sent)
    rest = exchange(merged, "samp", SAME_PAIR)
    given, rest = lax.optimization_barrier((given, rest))

    w_flip, w_last, _ = lax.optimization_barrier((out_flip, w_last, sent))
    w_next_flip, w_last_flip = to_seq(w_flip, (3, 0)), to_seq(w_flip, (1, 0))
    w_far = to_seq(w_last, (1, 0))

    row = jnp.arange(ROWS, dtype=jnp.int32)
    own_prompt = 256 * (row // 16) + 32 * slot + 16 * pair + row % 16
    position = jnp.where(row < PROMPT_ROWS, own_prompt, 2048 + pair) + prompt_offset[0]
    angles = position.astype(jnp.float32)[:, None] * rope_freqs(HEAD)[None, :]
    cosine, sine = jnp.cos(angles), jnp.sin(angles)
    cosine = jnp.concatenate([cosine, cosine], axis=1)
    sine = jnp.concatenate([-sine, sine], axis=1)
    queries, kv = rotate(mine, given, cosine, sine)
    all_kv = exchange(kv, "samp")
    *state, attended = attend_prefix(
        prefix_len, queries, pltpu.with_memory_space_constraint(key_value_cache, pltpu.HBM)
    )
    w_next_flip, _ = lax.optimization_barrier((w_next_flip, attended))
    w_far_flip = to_seq(w_next_flip, (3, 0))
    weights = [w_out, w_flip, w_next, w_next_flip, w_last, w_last_flip, w_far, w_far_flip]
    context = finish(queries, state, all_kv)
    context = context.reshape(SEQ * GROUPS, ROWS, HEAD)

    same = exchange(context, ("seq", "samp"), SEQ_GROUP)
    crossed = to_other_core(same)
    prompt_out, comp_out = output(rest, same, crossed, weights)
    return prompt_out, comp_out


def solution(mesh):
    placed = (
        P(),
        P(),
        P(),
        P(),
        P("seq", "samp"),
        P("samp"),
        P("samp", "seq"),
        P("seq", "samp"),
        P(None, "seq", None, None),
    )
    return jax.shard_map(
        body,
        mesh=mesh,
        in_specs=placed,
        out_specs=(P("seq", "samp"), P("seq", None, "samp")),
        check_vma=False,
    )
```

time: 334 us -> 305 us (0.913)
  blocking collectives: 37.7 us -> 0 us
  starting transfers between devices: 37.8 us -> 48.6 us
  local copies, waits for them, and re-layouts: 23.4 us -> 19.7 us
    ppermute x0 -> x4, waiting for transfers between devices: none -> 45.2 us  [the longest x3 45.2 us: to_ring(): return lax.ppermute(block, 'samp', pairs)]
    ppermute x7, waiting for transfers between devices: 130 us -> 85.5 us  [to_seq(): lax.ppermute(block, 'seq', [(i, moved(i, shift)) for i in range(SEQ)])]
    all_to_all x1 -> x0, blocking collectives: 37.7 us -> none  [exchange(): lax.all_to_all(blocks, axes, 0, 0, tiled=True, axis_index_groups=groups)]
    all_to_all x4 -> x5, starting transfers between devices: 27.5 us -> 34.3 us  [exchange(): lax.all_to_all(blocks, axes, 0, 0, tiled=True, axis_index_groups=groups)]
    ppermute x0 -> x4, starting transfers between devices: none -> 6.69 us  [the longest x3 3.71 us: to_ring(): return lax.ppermute(block, 'samp', pairs)]
    unnamed x25 -> x16, local copies, waits for them, and re-layouts: 9.02 us -> 4.53 us
    all_to_all x4 -> x5, waiting for transfers between devices: 52.1 us -> 53.2 us  [exchange(): lax.all_to_all(blocks, axes, 0, 0, tiled=True, axis_index_groups=groups)]
    pallas_call x2 -> x3, Pallas kernels: 9.28 us -> 10.1 us  [the longest x1 6.63 us: project(): pl.pallas_call(project_kernel, out_shape=(pltpu.HBM(shape, jnp.bfloat16),...]
  transfers between devices with their start and end apart: 14 -> 21, of which waited for: 9 -> 12; matrix products, arithmetic and copies ran while one was open for 1% -> 2% of each run, Pallas kernels for 6% -> 7%
where the time goes in v1:
time: 305 us; the launch traced here: 304 us
  waiting for transfers between devices  187 us (61%)
  starting transfers between devices  48.6 us (16%)
  Pallas kernels  42.5 us (14%)
  local copies, waits for them, and re-layouts  19.7 us (6%)
  other arithmetic  4.38 us (1%)
    ppermute x7, waiting for transfers between devices, to_seq(): lax.ppermute(block, 'seq', [(i, moved(i, shift)) for i in range(SEQ)])  85.5 us
    all_to_all x5, waiting for transfers between devices, exchange(): lax.all_to_all(blocks, axes, 0, 0, tiled=True, axis_index_groups=groups)  53.2 us
    ppermute x3, waiting for transfers between devices, to_ring(): return lax.ppermute(block, 'samp', pairs)  45.2 us
    all_to_all x5, starting transfers between devices, exchange(): lax.all_to_all(blocks, axes, 0, 0, tiled=True, axis_index_groups=groups)  34.3 us
    pallas_call x1, Pallas kernels, attend_prefix(): pl.pallas_call(functools.partial(prefix_kernel, slots=slots), out_shape=(...  19.2 us
    gather x1, local copies, waits for them, and re-layouts, body(): picked = embed_table.at[local].get(mode='promise_in_bounds')  11.6 us
    ppermute x7, starting transfers between devices, to_seq(): lax.ppermute(block, 'seq', [(i, moved(i, shift)) for i in range(SEQ)])  7.63 us
    pallas_call x1, Pallas kernels, project(): pl.pallas_call(project_kernel, out_shape=(pltpu.HBM(shape, jnp.bfloat16),...  6.63 us
  transfers between devices with their start and end apart: 21, of which 12 were waited for; matrix products, arithmetic and copies ran while one was open for 2% of the time, Pallas kernels for 7%

profile of v1, /device:TPU:6, one launch (start us, length us, event | category | flops | bytes accessed | tf_op | source)
XLA Modules:
  0.0 304.2 jit_solution(17944624470879580631)
XLA Ops:
  2.3 11.6 %gather_fusion = bf16[2176,512]{1,0:T(8,128)(2,1)S(1)} fusion(bf16[8016,512]{1,0:T(8,128)(2,1)} %param.13, s32[3072]{0:T(1024)S(1)} %pad_clamp_fusion), kind=kCustom, calls=%fused_computation | custom fusion | bytes 4465152 | tf_op jit(solution)/shard_map/gather | solution.py:517
  15.5 9.9 %all-to-all-start = ((bf16[64,136,128]{2,1,0:T(8,128)(2,1)}), bf16[64,136,128]{2,1,0:T(8,128)(2,1)S(1)}, u32[]{:S(2)}, u32[]{:S(2)}) async-start(bf16[64,136,128]{2,1,0:T(8,128)(2,1)} %arrange.1), calls=%async_computation | async-start | bytes 4456448 | tf_op jit(solution)/shard_map/all_to_all | solution.py:67
  27.0 2.8 collective-permute-start
  34.7 19.3 %all-to-all-done.got = bf16[64,136,128]{2,1,0:T(8,128)(2,1)S(1)} async-done(((bf16[64,136,128]{2,1,0:T(8,128)(2,1)}), bf16[64,136,128]{2,1,0:T(8,128)(2,1)S(1)}, u32[]{:S(2)}, u32[]{:S(2)}) %all-to-all-start) | async-done | bytes 2228256 | tf_op jit(solution)/shard_map/all_to_all | solution.py:67
  54.9 2.0 merge.1
  57.8 6.3 %all-to-all-start.1 = ((bf16[8,8,136,128]{3,2,1,0:T(8,128)(2,1)}), bf16[8,8,136,128]{3,2,1,0:T(8,128)(2,1)S(1)}, u32[]{:S(2)}, u32[]{:S(2)}) async-start(bf16[8,8,136,128]{3,2,1,0:T(8,128)(2,1)} %get-tuple-element.16), calls=%async_computation.1 | async-start | bytes 4456448 | tf_op jit(solution)/shard_map/all_to_all | solution.py:67
  64.1 16.1 %collective-permute-done.refs_1_ = bf16[512,1280]{1,0:T(8,128)(2,1)} collective-permute-done((bf16[512,1280]{1,0:T(8,128)(2,1)S(1)}, bf16[512,1280]{1,0:T(8,128)(2,1)}, u32[]{:S(2)}, u32[]{:S(2)}) %collective-permute-start) | collective-permute-done | bytes 1310752 | tf_op jit(solution)/shard_map/ppermute | solution.py:59
  80.9 28.4 %collective-permute-done.2.refs_3_ = bf16[512,1280]{1,0:T(8,128)(2,1)} collective-permute-done((bf16[512,1280]{1,0:T(8,128)(2,1)S(1)}, bf16[512,1280]{1,0:T(8,128)(2,1)}, u32[]{:S(2)}, u32[]{:S(2)}) %collective-permute-start.2) | collective-permute-done | bytes 1310752 | tf_op jit(solution)/shard_map/ppermute | solution.py:59
  110.1 2.7 collective-permute-done.6.refs_7_
  112.7 6.6 %project.1 = (bf16[136,1408]{1,0:T(8,128)(2,1)}, bf16[136,1408]{1,0:T(8,128)(2,1)}) custom-call(bf16[8,8,136,128]{3,2,1,0:T(8,128)(2,1)S(1)} %all-to-all-done.1.rows, bf16[512,1280]{1,0:T(8,128)(2,1)S(1)} %multiply_convert_fusion.refs_0_, bf16[512,1280]{1,0:T(8,128)(2,1)} %collective-permute-done.refs_1_, bf16[512,1280]{1,0:T(8,128)(2,1)} %collective-permute-done.1.refs_2_, ...), custom_call_target="tpu_custom_call" | custom-call | tf_op jit(solution)/shard_map/project/pallas_call | solution.py:218
  119.4 3.0 collective-permute-start.7
  122.4 3.4 %all-to-all-start.2 = ((bf16[8,136,128]{2,1,0:T(8,128)(2,1)}), bf16[8,136,128]{2,1,0:T(8,128)(2,1)S(1)}, u32[]{:S(2)}, u32[]{:S(2)}) async-start(bf16[8,136,128]{2,1,0:T(8,128)(2,1)} %get-tuple-element.19), calls=%async_computation.2 | async-start | bytes 557056 | tf_op jit(solution)/shard_map/all_to_all | solution.py:67
  126.3 7.2 %all-to-all-done.2.rest = bf16[8,136,128]{2,1,0:T(8,128)(2,1)S(1)} async-done(((bf16[8,136,128]{2,1,0:T(8,128)(2,1)}), bf16[8,136,128]{2,1,0:T(8,128)(2,1)S(1)}, u32[]{:S(2)}, u32[]{:S(2)}) %all-to-all-start.2) | async-done | bytes 278560 | tf_op jit(solution)/shard_map/all_to_all | solution.py:67
  136.0 3.9 %all-to-all-start.3 = ((bf16[16,136,256]{2,1,0:T(8,128)(2,1)}), bf16[16,136,256]{2,1,0:T(8,128)(2,1)S(1)}, u32[]{:S(2)}, u32[]{:S(2)}) async-start(bf16[16,136,256]{2,1,0:T(8,128)(2,1)} %get-tuple-element.27), calls=%async_computation.3 | async-start | bytes 2228224 | tf_op jit(solution)/shard_map/all_to_all | solution.py:67
  140.5 19.2 %prefix.1 = (f32[1088,128]{1,0:T(8,128)S(1)}, f32[1088,128]{1,0:T(8,128)S(1)}, f32[1088,128]{1,0:T(8,128)S(1)}, f32[8,128]{1,0:T(8,128)}) custom-call(s32[1]{0:T(128)S(6)} %copy.33.count, bf16[1088,128]{1,0:T(8,128)(2,1)S(1)} %get-tuple-element.23.q_ref, bf16[2,1,16384,128]{3,2,1,0:T(8,128)(2,1)} %kv_ref.1), custom_call_target="tpu_custom_call" | custom-call | tf_op jit(solution)/shard_map/prefix/pallas_call | solution.py:333
  161.6 6.0 %finish.1 = bf16[8,8,136,128]{3,2,1,0:T(8,128)(2,1)} custom-call(bf16[1088,128]{1,0:T(8,128)(2,1)S(1)} %get-tuple-element.23.q_ref, f32[1088,128]{1,0:T(8,128)S(1)} %get-tuple-element.24.acc_ref, f32[1088,128]{1,0:T(8,128)S(1)} %get-tuple-element.25.max_ref, f32[1088,128]{1,0:T(8,128)S(1)} %copy-done.2, bf16[16,136,256]{2,1,0:T(8,128)(2,1)S(1)} %all-to-all-done.3.kv), custom_call_target="tpu_custom_call" | custom-call | tf_op jit(solution)/shard_map/finish/pallas_call | solution.py:406
  167.7 10.8 %all-to-all-start.4 = ((bf16[64,136,128]{2,1,0:T(8,128)(2,1)}), bf16[64,136,128]{2,1,0:T(8,128)(2,1)S(1)}, u32[]{:S(2)}, u32[]{:S(2)}) async-start(bf16[64,136,128]{2,1,0:T(8,128)(2,1)} %bitcast.6), calls=%async_computation.4 | async-start | bytes 4456448 | tf_op jit(solution)/shard_map/all_to_all | solution.py:67
  180.9 26.8 %all-to-all-done.4.same = bf16[64,136,128]{2,1,0:T(8,128)(2,1)S(1)} async-done(((bf16[64,136,128]{2,1,0:T(8,128)(2,1)}), bf16[64,136,128]{2,1,0:T(8,128)(2,1)S(1)}, u32[]{:S(2)}, u32[]{:S(2)}) %all-to-all-start.4) | async-done | bytes 2228256 | tf_op jit(solution)/shard_map/all_to_all | solution.py:67
  207.6 18.4 %collective-permute-done.10.refs_4_ = bf16[1024,512]{1,0:T(8,128)(2,1)} collective-permute-done((bf16[1024,512]{1,0:T(8,128)(2,1)S(1)}, bf16[1024,512]{1,0:T(8,128)(2,1)}, u32[]{:S(2)}, u32[]{:S(2)}) %collective-permute-start.10) | collective-permute-done | bytes 1048608 | tf_op jit(solution)/shard_map/ppermute | solution.py:50
  229.7 1.7 collective-permute-start.13
  232.5 22.2 %collective-permute-done.12.refs_3_ = bf16[1024,512]{1,0:T(8,128)(2,1)S(1)} collective-permute-done((bf16[1024,512]{1,0:T(8,128)(2,1)}, bf16[1024,512]{1,0:T(8,128)(2,1)S(1)}, u32[]{:S(2)}, u32[]{:S(2)}) %collective-permute-start.12) | collective-permute-done | bytes 1048608 | tf_op jit(solution)/shard_map/ppermute | solution.py:50
  254.7 22.5 %collective-permute-done.11.refs_2_ = bf16[1024,512]{1,0:T(8,128)(2,1)S(1)} collective-permute-done((bf16[1024,512]{1,0:T(8,128)(2,1)S(1)}, bf16[1024,512]{1,0:T(8,128)(2,1)S(1)}, u32[]{:S(2)}, u32[]{:S(2)}) %collective-permute-start.11) | collective-permute-done | bytes 1048608 | tf_op jit(solution)/shard_map/ppermute | solution.py:50
  277.2 21.3 %collective-permute-done.15.refs_7_ = bf16[1024,512]{1,0:T(8,128)(2,1)S(1)} collective-permute-done((bf16[1024,512]{1,0:T(8,128)(2,1)S(1)}, bf16[1024,512]{1,0:T(8,128)(2,1)S(1)}, u32[]{:S(2)}, u32[]{:S(2)}) %collective-permute-start.15) | collective-permute-done | bytes 1048608 | tf_op jit(solution)/shard_map/ppermute | solution.py:50
  298.5 5.6 %output.1 = (bf16[256,512]{1,0:T(8,128)(2,1)}, bf16[8,2,512]{2,1,0:T(2,128)(2,1)}) custom-call(bf16[8,136,128]{2,1,0:T(8,128)(2,1)S(1)} %all-to-all-done.2.rest, bf16[64,136,128]{2,1,0:T(8,128)(2,1)S(1)} %all-to-all-done.4.same, bf16[64,136,128]{2,1,0:T(8,128)(2,1)S(1)} %collective-permute-done.8.crossed, bf16[1024,512]{1,0:T(8,128)(2,1)S(1)} %copy-done, ...), custom_call_target="tpu_custom_call" | custom-call | tf_op jit(solution)/shard_map/output/pallas_call | solution.py:476
  (63 shorter events, 24.3 us)
Async XLA Ops:
  15.4 9.9 %copy-start.6 = (bf16[512]{0:T(512)(128)(2,1)S(1)}, bf16[512]{0:T(512)(128)(2,1)}, u32[]{:S(2)}) copy-start(bf16[512]{0:T(512)(128)(2,1)} %param.14) | copy-start | bytes 3076
  15.5 38.5 %all-to-all-start = ((bf16[64,136,128]{2,1,0:T(8,128)(2,1)}), bf16[64,136,128]{2,1,0:T(8,128)(2,1)S(1)}, u32[]{:S(2)}, u32[]{:S(2)}) async-start(bf16[64,136,128]{2,1,0:T(8,128)(2,1)} %arrange.1), calls=%async_computation | async-start | bytes 4456448 | tf_op jit(solution)/shard_map/all_to_all | solution.py:67
  27.0 53.2 %collective-permute-start = (bf16[512,1280]{1,0:T(8,128)(2,1)S(1)}, bf16[512,1280]{1,0:T(8,128)(2,1)}, u32[]{:S(2)}, u32[]{:S(2)}) collective-permute-start(bf16[512,1280]{1,0:T(8,128)(2,1)S(1)} %multiply_convert_fusion.refs_0_), channel_id=1, source_target_pairs={{0,6},{1,7},{2,0},{3,1},{4,2},{5,3},{6,4},{7,5},{8,14},{9,15},{10,... | collective-permute-start | bytes 3932168 | tf_op jit(solution)/shard_map/ppermute | solution.py:59
  29.7 51.2 %collective-permute-start.1 = (bf16[512,1280]{1,0:T(8,128)(2,1)S(1)}, bf16[512,1280]{1,0:T(8,128)(2,1)}, u32[]{:S(2)}, u32[]{:S(2)}) collective-permute-start(bf16[512,1280]{1,0:T(8,128)(2,1)S(1)} %multiply_convert_fusion.refs_0_), channel_id=1, source_target_pairs={{0,2},{1,3},{2,4},{3,5},{4,6},{5,7},{6,0},{7,1},{8,10},{9,11},{10,... | collective-permute-start | bytes 3932168 | tf_op jit(solution)/shard_map/ppermute | solution.py:59
  56.9 52.5 %collective-permute-start.2 = (bf16[512,1280]{1,0:T(8,128)(2,1)S(1)}, bf16[512,1280]{1,0:T(8,128)(2,1)}, u32[]{:S(2)}, u32[]{:S(2)}) collective-permute-start(bf16[512,1280]{1,0:T(8,128)(2,1)S(1)} %multiply_convert_fusion.refs_0_), channel_id=1, source_target_pairs={{0,4},{1,5},{2,6},{3,7},{4,0},{5,1},{6,2},{7,3},{8,12},{9,13},{10,... | collective-permute-start | bytes 3932168 | tf_op jit(solution)/shard_map/ppermute | solution.py:59
  57.8 52.3 %all-to-all-start.1 = ((bf16[8,8,136,128]{3,2,1,0:T(8,128)(2,1)}), bf16[8,8,136,128]{3,2,1,0:T(8,128)(2,1)S(1)}, u32[]{:S(2)}, u32[]{:S(2)}) async-start(bf16[8,8,136,128]{3,2,1,0:T(8,128)(2,1)} %get-tuple-element.16), calls=%async_computation.1 | async-start | bytes 4456448 | tf_op jit(solution)/shard_map/all_to_all | solution.py:67
  64.1 45.9 %collective-permute-start.3 = (bf16[512,1280]{1,0:T(8,128)(2,1)S(1)}, bf16[512,1280]{1,0:T(8,128)(2,1)}, u32[]{:S(2)}, u32[]{:S(2)}) collective-permute-start(bf16[512,1280]{1,0:T(8,128)(2,1)S(1)} %multiply_convert_fusion.refs_0_), channel_id=1, source_target_pairs={{0,1},{1,0},{2,3},{3,2},{4,5},{5,4},{6,7},{7,6},{8,9},{9,8},{10,11... | collective-permute-start | bytes 3932168 | tf_op jit(solution)/shard_map/ppermute | solution.py:54
  80.2 29.9 %collective-permute-start.4 = (bf16[512,1280]{1,0:T(8,128)(2,1)}, bf16[512,1280]{1,0:T(8,128)(2,1)}, u32[]{:S(2)}, u32[]{:S(2)}) collective-permute-start(bf16[512,1280]{1,0:T(8,128)(2,1)} %collective-permute-done.refs_1_), channel_id=1, source_target_pairs={{0,1},{1,0},{2,3},{3,2},{4,5},{5,4},{6,7},{7,6},{8,9},{9,8},{10,11... | collective-permute-start | bytes 3932168 | tf_op jit(solution)/shard_map/ppermute | solution.py:54
  80.9 29.1 %collective-permute-start.5 = (bf16[512,1280]{1,0:T(8,128)(2,1)}, bf16[512,1280]{1,0:T(8,128)(2,1)}, u32[]{:S(2)}, u32[]{:S(2)}) collective-permute-start(bf16[512,1280]{1,0:T(8,128)(2,1)} %collective-permute-done.1.refs_2_), channel_id=1, source_target_pairs={{0,1},{1,0},{2,3},{3,2},{4,5},{5,4},{6,7},{7,6},{8,9},{9,8},{10,11... | collective-permute-start | bytes 3932168 | tf_op jit(solution)/shard_map/ppermute | solution.py:54
  109.4 3.4 %collective-permute-start.6 = (bf16[512,1280]{1,0:T(8,128)(2,1)}, bf16[512,1280]{1,0:T(8,128)(2,1)}, u32[]{:S(2)}, u32[]{:S(2)}) collective-permute-start(bf16[512,1280]{1,0:T(8,128)(2,1)} %collective-permute-done.2.refs_3_), channel_id=1, source_target_pairs={{0,1},{1,0},{2,3},{3,2},{4,5},{5,4},{6,7},{7,6},{8,9},{9,8},{10,11... | collective-permute-start | bytes 3932168 | tf_op jit(solution)/shard_map/ppermute | solution.py:54
  119.4 14.1 %collective-permute-start.7 = (bf16[136,1408]{1,0:T(8,128)(2,1)}, bf16[136,1408]{1,0:T(8,128)(2,1)S(1)}, u32[]{:S(2)}, u32[]{:S(2)}) collective-permute-start(bf16[136,1408]{1,0:T(8,128)(2,1)} %get-tuple-element.18), channel_id=1, source_target_pairs={{0,8},{1,9},{2,10},{3,11},{4,12},{5,13},{6,14},{7,15},{8,0},{9,1},... | collective-permute-start | bytes 1148936 | tf_op jit(solution)/shard_map/ppermute | solution.py:63
  122.4 11.0 %all-to-all-start.2 = ((bf16[8,136,128]{2,1,0:T(8,128)(2,1)}), bf16[8,136,128]{2,1,0:T(8,128)(2,1)S(1)}, u32[]{:S(2)}, u32[]{:S(2)}) async-start(bf16[8,136,128]{2,1,0:T(8,128)(2,1)} %get-tuple-element.19), calls=%async_computation.2 | async-start | bytes 557056 | tf_op jit(solution)/shard_map/all_to_all | solution.py:67
  136.0 24.6 %all-to-all-start.3 = ((bf16[16,136,256]{2,1,0:T(8,128)(2,1)}), bf16[16,136,256]{2,1,0:T(8,128)(2,1)S(1)}, u32[]{:S(2)}, u32[]{:S(2)}) async-start(bf16[16,136,256]{2,1,0:T(8,128)(2,1)} %get-tuple-element.27), calls=%async_computation.3 | async-start | bytes 2228224 | tf_op jit(solution)/shard_map/all_to_all | solution.py:67
  160.6 1.1 copy-start.2
  167.7 10.8 %copy-start = (bf16[1024,512]{1,0:T(8,128)(2,1)S(1)}, bf16[1024,512]{1,0:T(8,128)(2,1)}, u32[]{:S(2)}) copy-start(bf16[1024,512]{1,0:T(8,128)(2,1)} %refs_0_.1) | copy-start | bytes 3145732
  167.7 39.9 %all-to-all-start.4 = ((bf16[64,136,128]{2,1,0:T(8,128)(2,1)}), bf16[64,136,128]{2,1,0:T(8,128)(2,1)S(1)}, u32[]{:S(2)}, u32[]{:S(2)}) async-start(bf16[64,136,128]{2,1,0:T(8,128)(2,1)} %bitcast.6), calls=%async_computation.4 | async-start | bytes 4456448 | tf_op jit(solution)/shard_map/all_to_all | solution.py:67
  178.5 47.5 %collective-permute-start.10 = (bf16[1024,512]{1,0:T(8,128)(2,1)S(1)}, bf16[1024,512]{1,0:T(8,128)(2,1)}, u32[]{:S(2)}, u32[]{:S(2)}) collective-permute-start(bf16[1024,512]{1,0:T(8,128)(2,1)S(1)} %copy-done), channel_id=1, source_target_pairs={{0,16},{16,32},{32,48},{48,0},{64,80},{80,96},{96,112},{112,64},{1... | collective-permute-start | bytes 3145736 | tf_op jit(solution)/shard_map/ppermute | solution.py:50
  179.2 48.0 %collective-permute-start.9 = (bf16[1024,512]{1,0:T(8,128)(2,1)S(1)}, bf16[1024,512]{1,0:T(8,128)(2,1)}, u32[]{:S(2)}, u32[]{:S(2)}) collective-permute-start(bf16[1024,512]{1,0:T(8,128)(2,1)S(1)} %copy-done), channel_id=1, source_target_pairs={{0,64},{16,80},{32,96},{48,112},{64,0},{80,16},{96,32},{112,48},{1... | collective-permute-start | bytes 3145736 | tf_op jit(solution)/shard_map/ppermute | solution.py:50
  207.6 90.8 %collective-permute-start.8 = (bf16[64,136,128]{2,1,0:T(8,128)(2,1)S(1)}, bf16[64,136,128]{2,1,0:T(8,128)(2,1)S(1)}, u32[]{:S(2)}, u32[]{:S(2)}) collective-permute-start(bf16[64,136,128]{2,1,0:T(8,128)(2,1)S(1)} %all-to-all-done.4.same), channel_id=1, source_target_pairs={{0,1},{1,0},{2,3},{3,2},{4,5},{5,4},{6,7},{7,6},{8,9},{9,8},{10,11... | collective-permute-start | bytes 6684680 | tf_op jit(solution)/shard_map/ppermute | solution.py:54
  227.2 27.5 %collective-permute-start.12 = (bf16[1024,512]{1,0:T(8,128)(2,1)}, bf16[1024,512]{1,0:T(8,128)(2,1)S(1)}, u32[]{:S(2)}, u32[]{:S(2)}) collective-permute-start(bf16[1024,512]{1,0:T(8,128)(2,1)} %collective-permute-done.9.refs_1_), channel_id=1, source_target_pairs={{0,48},{16,0},{32,16},{48,32},{64,112},{80,64},{96,80},{112,96},{1... | collective-permute-start | bytes 3145736 | tf_op jit(solution)/shard_map/ppermute | solution.py:50
  228.2 49.0 %collective-permute-start.11 = (bf16[1024,512]{1,0:T(8,128)(2,1)S(1)}, bf16[1024,512]{1,0:T(8,128)(2,1)S(1)}, u32[]{:S(2)}, u32[]{:S(2)}) collective-permute-start(bf16[1024,512]{1,0:T(8,128)(2,1)S(1)} %copy-done), channel_id=1, source_target_pairs={{0,48},{16,0},{32,16},{48,32},{64,112},{80,64},{96,80},{112,96},{1... | collective-permute-start | bytes 3145736 | tf_op jit(solution)/shard_map/ppermute | solution.py:50
  229.7 47.5 %collective-permute-start.13 = (bf16[1024,512]{1,0:T(8,128)(2,1)}, bf16[1024,512]{1,0:T(8,128)(2,1)S(1)}, u32[]{:S(2)}, u32[]{:S(2)}) collective-permute-start(bf16[1024,512]{1,0:T(8,128)(2,1)} %collective-permute-done.9.refs_1_), channel_id=1, source_target_pairs={{0,16},{16,32},{32,48},{48,0},{64,80},{80,96},{96,112},{112,64},{1... | collective-permute-start | bytes 3145736 | tf_op jit(solution)/shard_map/ppermute | solution.py:50
  231.4 45.7 %collective-permute-start.14 = (bf16[1024,512]{1,0:T(8,128)(2,1)}, bf16[1024,512]{1,0:T(8,128)(2,1)S(1)}, u32[]{:S(2)}, u32[]{:S(2)}) collective-permute-start(bf16[1024,512]{1,0:T(8,128)(2,1)} %collective-permute-done.10.refs_4_), channel_id=1, source_target_pairs={{0,16},{16,32},{32,48},{48,0},{64,80},{80,96},{96,112},{112,64},{1... | collective-permute-start | bytes 3145736 | tf_op jit(solution)/shard_map/ppermute | solution.py:50
  254.7 43.8 %collective-permute-start.15 = (bf16[1024,512]{1,0:T(8,128)(2,1)S(1)}, bf16[1024,512]{1,0:T(8,128)(2,1)S(1)}, u32[]{:S(2)}, u32[]{:S(2)}) collective-permute-start(bf16[1024,512]{1,0:T(8,128)(2,1)S(1)} %collective-permute-done.12.refs_3_), channel_id=1, source_target_pairs={{0,48},{16,0},{32,16},{48,32},{64,112},{80,64},{96,80},{112,96},{1... | collective-permute-start | bytes 3145736 | tf_op jit(solution)/shard_map/ppermute | solution.py:50
  (4 other events, 3.6 us)

commit v2 on v1

--- a/solution.py
+++ b/solution.py
@@ -69,6 +69,10 @@
 
 def whole(memory_space=pltpu.VMEM):
     return pl.BlockSpec(memory_space=memory_space)
+
+
+def in_hbm(block):
+    return pltpu.with_memory_space_constraint(block, pltpu.HBM)
 
 
 def selection(rows, columns, wanted):
@@ -121,7 +125,10 @@
     )(picked)
 
 
-def merge_kernel(got, owner, copies, merged, held, sem):
+def merge_kernel(got, owners, copies, merged, held, owner, sem):
+    load = pltpu.make_async_copy(owners, owner, sem.at[SEQ + 1])
+    load.start()
+    load.wait()
     sends = [pltpu.make_async_copy(held, copies.at[s], sem.at[s]) for s in range(SEQ)]
     sends.append(pltpu.make_async_copy(held, merged, sem.at[SEQ]))
     owns = [owner[...] == s for s in range(SEQ)]
@@ -143,15 +150,16 @@
             pltpu.HBM((SEQ, SLOTS, ROWS, HEAD), jnp.bfloat16),
             pltpu.HBM((SLOTS, ROWS, HEAD), jnp.bfloat16),
         ),
-        in_specs=[whole(), whole()],
+        in_specs=[whole(), whole(pl.ANY)],
         out_specs=(whole(pltpu.HBM), whole(pltpu.HBM)),
         scratch_shapes=[
             pltpu.VMEM((SLOTS, ROWS, HEAD), jnp.bfloat16),
-            pltpu.SemaphoreType.DMA((SEQ + 1,)),
+            pltpu.VMEM((ROWS, 1), jnp.int32),
+            pltpu.SemaphoreType.DMA((SEQ + 2,)),
         ],
         compiler_params=pltpu.CompilerParams(vmem_limit_bytes=16 << 20),
         name="merge",
-    )(got, owner)
+    )(got, in_hbm(owner))
 
 
 def project_kernel(rows, *refs):
@@ -277,10 +285,10 @@
         ],
         compiler_params=pltpu.CompilerParams(vmem_limit_bytes=16 << 20),
         name="rotate",
-    )(mine, given, cosine, sine)
-
-
-def prefix_kernel(count, q_ref, kv_ref, acc_ref, max_ref, sum_ref, token_ref, *, slots):
+    )(in_hbm(mine), given, cosine, sine)
+
+
+def prefix_kernel(count, q_ref, kv_ref, acc_out, stat_out, acc_ref, max_ref, sum_ref, sem, *, slots):
     step = pl.program_id(0)
 
     @pl.when(step == 0)
@@ -288,7 +296,6 @@
         acc_ref[...] = jnp.zeros_like(acc_ref)
         max_ref[...] = jnp.full_like(max_ref, MASK_FILL)
         sum_ref[...] = jnp.zeros_like(sum_ref)
-        token_ref[...] = jnp.zeros_like(token_ref)
 
     first = step * slots
 
@@ -322,17 +329,30 @@
     def _():
         absorb(True)
 
+    @pl.when(step == pl.num_programs(0) - 1)
+    def _():
+        lane = lax.broadcasted_iota(jnp.int32, max_ref.shape, 1)
+        max_ref[...] = jnp.where(lane < HEAD // 2, max_ref[...], sum_ref[...])
+        sends = [
+            pltpu.make_async_copy(acc_ref, acc_out, sem.at[0]),
+            pltpu.make_async_copy(max_ref, stat_out, sem.at[1]),
+        ]
+        for send in sends:
+            send.start()
+        for send in sends:
+            send.wait()
+
 
 def attend_prefix(count, queries, cache, slots=2048):
     n = queries.shape[0]
-    state = jax.ShapeDtypeStruct((n, HEAD), jnp.float32)
+    state = pltpu.HBM((n, HEAD), jnp.float32)
 
     def cache_block(step, count):
         return (0, 0, jnp.minimum(step, lax.div(count[0] - 1, slots)), 0)
 
     return pl.pallas_call(
         functools.partial(prefix_kernel, slots=slots),
-        out_shape=(state, state, state, jax.ShapeDtypeStruct((8, HEAD), jnp.float32)),
+        out_shape=(state, state),
         grid_spec=pltpu.PrefetchScalarGridSpec(
             num_scalar_prefetch=1,
             grid=(cache.shape[2] // slots,),
@@ -340,17 +360,24 @@
                 pl.BlockSpec((n, HEAD), lambda step, count: (0, 0)),
                 pl.BlockSpec((2, 1, slots, HEAD), cache_block),
             ],
-            out_specs=[pl.BlockSpec((n, HEAD), lambda step, count: (0, 0))] * 3
-            + [pl.BlockSpec((8, HEAD), lambda step, count: (0, 0))],
+            out_specs=[whole(pltpu.HBM)] * 2,
+            scratch_shapes=[pltpu.VMEM((n, HEAD), jnp.float32)] * 3
+            + [pltpu.SemaphoreType.DMA((2,))],
         ),
         compiler_params=pltpu.CompilerParams(
-            dimension_semantics=("arbitrary",), vmem_limit_bytes=14 << 20
+            dimension_semantics=("arbitrary",), vmem_limit_bytes=16 << 20
         ),
         name="prefix",
     )(count, queries, cache)
 
 
-def finish_kernel(q_ref, acc_ref, max_ref, sum_ref, kv, out, block, comp_block, sem):
+def finish_kernel(q_ref, acc_in, stat_in, kv, out, block, comp_block, acc_ref, stat_ref, sem):
+    loads = [
+        pltpu.make_async_copy(acc_in, acc_ref, sem.at[GROUPS]),
+        pltpu.make_async_copy(stat_in, stat_ref, sem.at[GROUPS + 1]),
+    ]
+    for load in loads:
+        load.start()
     samp_index = lax.axis_index("samp")
     pair, slot = samp_index // 8, samp_index % 8
     keys = jnp.concatenate([kv[m, :PROMPT_ROWS, :HEAD] for m in range(SAMP)], axis=0)
@@ -369,6 +396,8 @@
     column = lax.broadcasted_iota(jnp.int32, (1, 2 * SEQ), 1)
     live = (column % SEQ == row - PROMPT_ROWS) & (column // SEQ <= pair)
     comp_bias = jnp.where(live, 0.0, MASK_FILL)
+    for load in loads:
+        load.wait()
     for h in range(HEADS):
         rows = pl.ds(h * ROWS, ROWS)
         q = q_ref[rows, :]
@@ -377,7 +406,7 @@
             lax.dot_general(q, comp[:, :HEAD], LAST_DIMS, preferred_element_type=jnp.float32)
             + comp_bias
         )
-        old = max_ref[rows, :]
+        old, old_sum = stat_ref[rows, :1], stat_ref[rows, HEAD // 2 : HEAD // 2 + 1]
         new = jnp.maximum(old, jnp.max(scores, axis=1, keepdims=True))
         new = jnp.maximum(new, jnp.max(comp_scores, axis=1, keepdims=True))
         weights = jnp.exp2(scores - new[:, :1]).astype(jnp.bfloat16)
@@ -386,7 +415,7 @@
         both = jnp.dot(weights, values, preferred_element_type=jnp.float32)
         both = both + jnp.dot(comp_weights, comp_values, preferred_element_type=jnp.float32)
         context = acc_ref[rows, :] * factor + both[:, :HEAD]
-        context = context / (sum_ref[rows, :] * factor + both[:, HEAD:])
+        context = context / (old_sum * factor + both[:, HEAD:])
         for s in range(SEQ):
             block[s, pl.ds(16 * h, 16), :] = context[16 * s : 16 * s + 16].astype(jnp.bfloat16)
             comp_block[s, pl.ds(h, 1), :] = context[PROMPT_ROWS + s : PROMPT_ROWS + s + 1]
@@ -406,16 +435,18 @@
     return pl.pallas_call(
         finish_kernel,
         out_shape=pltpu.HBM((SEQ, GROUPS, ROWS, HEAD), jnp.bfloat16),
-        in_specs=[whole()] * 5,
+        in_specs=[whole(), whole(pl.ANY), whole(pl.ANY), whole()],
         out_specs=whole(pltpu.HBM),
         scratch_shapes=[
             pltpu.VMEM((SEQ, ROWS, HEAD), jnp.bfloat16),
             pltpu.VMEM((SEQ, HEADS, HEAD), jnp.float32),
-            pltpu.SemaphoreType.DMA((GROUPS,)),
+            pltpu.VMEM(queries.shape, jnp.float32),
+            pltpu.VMEM(queries.shape, jnp.float32),
+            pltpu.SemaphoreType.DMA((GROUPS + 2,)),
         ],
-        compiler_params=pltpu.CompilerParams(vmem_limit_bytes=14 << 20),
+        compiler_params=pltpu.CompilerParams(vmem_limit_bytes=16 << 20),
         name="finish",
-    )(queries, *state, kv)
+    )(queries, *(in_hbm(block) for block in state), kv)
 
 
 def output_kernel(rest, same, crossed, *refs):
@@ -529,14 +560,14 @@
     scaled_far = to_ring(by_ring, 2)
     scales = [scaled, scaled_next, scaled_last, scaled_far]
     scales = scales + [to_other_core(w) for w in scales]
+    w_flip, w_last, _ = lax.optimization_barrier((out_flip, w_last, scaled_far))
+    w_next_flip, w_last_flip = to_seq(w_flip, (3, 0)), to_seq(w_flip, (1, 0))
+    w_far = to_seq(w_last, (1, 0))
+
     mine, sent = project(rows, scales)
     given = to_other_pair(sent)
     rest = exchange(merged, "samp", SAME_PAIR)
     given, rest = lax.optimization_barrier((given, rest))
-
-    w_flip, w_last, _ = lax.optimization_barrier((out_flip, w_last, sent))
-    w_next_flip, w_last_flip = to_seq(w_flip, (3, 0)), to_seq(w_flip, (1, 0))
-    w_far = to_seq(w_last, (1, 0))
 
     row = jnp.arange(ROWS, dtype=jnp.int32)
     own_prompt = 256 * (row // 16) + 32 * slot + 16 * pair + row % 16
@@ -547,11 +578,11 @@
     sine = jnp.concatenate([-sine, sine], axis=1)
     queries, kv = rotate(mine, given, cosine, sine)
     all_kv = exchange(kv, "samp")
-    *state, attended = attend_prefix(
+    queries, w_next_flip = lax.optimization_barrier((queries, w_next_flip))
+    w_far_flip = to_seq(w_next_flip, (3, 0))
+    state = attend_prefix(
         prefix_len, queries, pltpu.with_memory_space_constraint(key_value_cache, pltpu.HBM)
     )
-    w_next_flip, _ = lax.optimization_barrier((w_next_flip, attended))
-    w_far_flip = to_seq(w_next_flip, (3, 0))
     weights = [w_out, w_flip, w_next, w_next_flip, w_last, w_last_flip, w_far, w_far_flip]
     context = finish(queries, state, all_kv)
     context = context.reshape(SEQ * GROUPS, ROWS, HEAD)

time: 305 us -> 285 us (0.934); the launches traced: 304 us -> 280 us
  waiting for transfers between devices: 187 us -> 138 us
  blocking collectives: 0 us -> 36.4 us
  starting transfers between devices: 48.6 us -> 37.9 us
  local copies, waits for them, and re-layouts: 19.7 us -> 15.9 us
    all_to_all x0 -> x1, blocking collectives: none -> 36.4 us  [exchange(): lax.all_to_all(blocks, axes, 0, 0, tiled=True, axis_index_groups=groups)]
    all_to_all x5 -> x4, waiting for transfers between devices: 53.2 us -> 19.3 us  [exchange(): lax.all_to_all(blocks, axes, 0, 0, tiled=True, axis_index_groups=groups)]
    ppermute x7, waiting for transfers between devices: 85.5 us -> 64.6 us  [to_seq(): lax.ppermute(block, 'seq', [(i, moved(i, shift)) for i in range(SEQ)])]
    all_to_all x5 -> x4, starting transfers between devices: 34.3 us -> 23 us  [exchange(): lax.all_to_all(blocks, axes, 0, 0, tiled=True, axis_index_groups=groups)]
    ppermute x1, waiting for transfers between devices: 0.01 us -> 8.58 us  [to_other_pair(): lax.ppermute(block, 'samp', [(m, (m + 8) % SAMP) for m in range(SAMP)])]
    unnamed x16 -> x8, local copies, waits for them, and re-layouts: 4.53 us -> 0.79 us
  transfers between devices with their start and end apart: 21 -> 20, of which waited for: 12 -> 12; matrix products, arithmetic and copies ran while one was open for 2% -> 3% of each run, Pallas kernels for 7% -> 11%
where the time goes in v2:
time: 285 us; the launch traced here: 280 us
  waiting for transfers between devices  138 us (48%)
  Pallas kernels  45.2 us (16%)
  starting transfers between devices  37.9 us (13%)
  blocking collectives  36.4 us (13%)
  local copies, waits for them, and re-layouts  15.9 us (6%)
  other arithmetic  4.37 us (2%)
    ppermute x7, waiting for transfers between devices, to_seq(): lax.ppermute(block, 'seq', [(i, moved(i, shift)) for i in range(SEQ)])  64.6 us
    ppermute x3, waiting for transfers between devices, to_ring(): return lax.ppermute(block, 'samp', pairs)  45.2 us
    all_to_all x1, blocking collectives, exchange(): lax.all_to_all(blocks, axes, 0, 0, tiled=True, axis_index_groups=groups)  36.4 us
    all_to_all x4, starting transfers between devices, exchange(): lax.all_to_all(blocks, axes, 0, 0, tiled=True, axis_index_groups=groups)  23 us
    pallas_call x1, Pallas kernels, attend_prefix(): pl.pallas_call(functools.partial(prefix_kernel, slots=slots), out_shape=(...  19.4 us
    all_to_all x4, waiting for transfers between devices, exchange(): lax.all_to_all(blocks, axes, 0, 0, tiled=True, axis_index_groups=groups)  19.3 us
    gather x1, local copies, waits for them, and re-layouts, body(): picked = embed_table.at[local].get(mode='promise_in_bounds')  11.6 us
    ppermute x1, waiting for transfers between devices, to_other_pair(): lax.ppermute(block, 'samp', [(m, (m + 8) % SAMP) for m in range(SAMP)])  8.58 us
  transfers between devices with their start and end apart: 20, of which 12 were waited for; matrix products, arithmetic and copies ran while one was open for 3% of the time, Pallas kernels for 11%

profile of v2, /device:TPU:6, one launch (start us, length us, event | category | flops | bytes accessed | tf_op | source)
XLA Modules:
  0.0 280.4 jit_solution(11011735306653030749)
XLA Ops:
  2.3 11.6 %gather_fusion = bf16[2176,512]{1,0:T(8,128)(2,1)S(1)} fusion(bf16[8016,512]{1,0:T(8,128)(2,1)} %param.13, s32[3072]{0:T(1024)S(1)} %pad_clamp_fusion), kind=kCustom, calls=%fused_computation | custom fusion | bytes 4465152 | tf_op jit(solution)/shard_map/gather | solution.py:548
  15.4 9.9 %all-to-all-start = ((bf16[64,136,128]{2,1,0:T(8,128)(2,1)}), bf16[64,136,128]{2,1,0:T(8,128)(2,1)S(1)}, u32[]{:S(2)}, u32[]{:S(2)}) async-start(bf16[64,136,128]{2,1,0:T(8,128)(2,1)} %arrange.1), calls=%async_computation | async-start | bytes 4456448 | tf_op jit(solution)/shard_map/all_to_all | solution.py:67
  26.9 2.8 collective-permute-start
  34.7 19.3 %all-to-all-done.got = bf16[64,136,128]{2,1,0:T(8,128)(2,1)S(1)} async-done(((bf16[64,136,128]{2,1,0:T(8,128)(2,1)}), bf16[64,136,128]{2,1,0:T(8,128)(2,1)S(1)}, u32[]{:S(2)}, u32[]{:S(2)}) %all-to-all-start) | async-done | bytes 2228256 | tf_op jit(solution)/shard_map/all_to_all | solution.py:67
  54.0 2.9 %merge.1 = (bf16[8,8,136,128]{3,2,1,0:T(8,128)(2,1)}, bf16[8,136,128]{2,1,0:T(8,128)(2,1)}) custom-call(bf16[64,136,128]{2,1,0:T(8,128)(2,1)S(1)} %all-to-all-done.got, s32[136,1]{1,0:T(8,128)} %add_select_fusion.owners), custom_call_target="tpu_custom_call" | custom-call | tf_op jit(solution)/shard_map/merge/pallas_call | solution.py:147
  58.2 6.0 %all-to-all-start.1 = ((bf16[8,8,136,128]{3,2,1,0:T(8,128)(2,1)}), bf16[8,8,136,128]{3,2,1,0:T(8,128)(2,1)S(1)}, u32[]{:S(2)}, u32[]{:S(2)}) async-start(bf16[8,8,136,128]{3,2,1,0:T(8,128)(2,1)} %get-tuple-element.17), calls=%async_computation.1 | async-start | bytes 4456448 | tf_op jit(solution)/shard_map/all_to_all | solution.py:67
  64.1 16.0 %collective-permute-done.refs_1_ = bf16[512,1280]{1,0:T(8,128)(2,1)} collective-permute-done((bf16[512,1280]{1,0:T(8,128)(2,1)S(1)}, bf16[512,1280]{1,0:T(8,128)(2,1)}, u32[]{:S(2)}, u32[]{:S(2)}) %collective-permute-start) | collective-permute-done | bytes 1310752 | tf_op jit(solution)/shard_map/ppermute | solution.py:59
  80.9 28.4 %collective-permute-done.2.refs_3_ = bf16[512,1280]{1,0:T(8,128)(2,1)} collective-permute-done((bf16[512,1280]{1,0:T(8,128)(2,1)S(1)}, bf16[512,1280]{1,0:T(8,128)(2,1)}, u32[]{:S(2)}, u32[]{:S(2)}) %collective-permute-start.2) | collective-permute-done | bytes 1310752 | tf_op jit(solution)/shard_map/ppermute | solution.py:59
  109.3 2.0 collective-permute-start.8
  112.7 6.6 %project.1 = (bf16[136,1408]{1,0:T(8,128)(2,1)}, bf16[136,1408]{1,0:T(8,128)(2,1)}) custom-call(bf16[8,8,136,128]{3,2,1,0:T(8,128)(2,1)S(1)} %all-to-all-done.1.rows, bf16[512,1280]{1,0:T(8,128)(2,1)S(1)} %multiply_convert_fusion.refs_0_, bf16[512,1280]{1,0:T(8,128)(2,1)} %collective-permute-done.refs_1_, bf16[512,1280]{1,0:T(8,128)(2,1)} %collective-permute-done.1.refs_2_, ...), custom_call_target="tpu_custom_call" | custom-call | tf_op jit(solution)/shard_map/project/pallas_call | solution.py:226
  119.3 3.0 %collective-permute-start.7 = (bf16[136,1408]{1,0:T(8,128)(2,1)}, bf16[136,1408]{1,0:T(8,128)(2,1)S(1)}, u32[]{:S(2)}, u32[]{:S(2)}) collective-permute-start(bf16[136,1408]{1,0:T(8,128)(2,1)} %get-tuple-element.19), channel_id=1, source_target_pairs={{0,8},{1,9},{2,10},{3,11},{4,12},{5,13},{6,14},{7,15},{8,0},{9,1},... | collective-permute-start | bytes 1148936 | tf_op jit(solution)/shard_map/ppermute | solution.py:63
  122.3 3.4 %all-to-all-start.2 = ((bf16[8,136,128]{2,1,0:T(8,128)(2,1)}), bf16[8,136,128]{2,1,0:T(8,128)(2,1)S(1)}, u32[]{:S(2)}, u32[]{:S(2)}) async-start(bf16[8,136,128]{2,1,0:T(8,128)(2,1)} %get-tuple-element.20), calls=%async_computation.2 | async-start | bytes 557056 | tf_op jit(solution)/shard_map/all_to_all | solution.py:67
  126.1 9.6 %collective-permute-done.8.refs_1_ = bf16[1024,512]{1,0:T(8,128)(2,1)} collective-permute-done((bf16[1024,512]{1,0:T(8,128)(2,1)}, bf16[1024,512]{1,0:T(8,128)(2,1)}, u32[]{:S(2)}, u32[]{:S(2)}) %collective-permute-start.8) | collective-permute-done | bytes 1048608 | tf_op jit(solution)/shard_map/ppermute | solution.py:50
  137.6 8.6 %collective-permute-done.7.given = bf16[136,1408]{1,0:T(8,128)(2,1)S(1)} collective-permute-done((bf16[136,1408]{1,0:T(8,128)(2,1)}, bf16[136,1408]{1,0:T(8,128)(2,1)S(1)}, u32[]{:S(2)}, u32[]{:S(2)}) %collective-permute-start.7) | collective-permute-done | bytes 383008 | tf_op jit(solution)/shard_map/ppermute | solution.py:63
  146.2 2.4 rotate.1
  148.6 3.7 %all-to-all-start.3 = ((bf16[16,136,256]{2,1,0:T(8,128)(2,1)}), bf16[16,136,256]{2,1,0:T(8,128)(2,1)S(1)}, u32[]{:S(2)}, u32[]{:S(2)}) async-start(bf16[16,136,256]{2,1,0:T(8,128)(2,1)} %get-tuple-element.29), calls=%async_computation.3 | async-start | bytes 2228224 | tf_op jit(solution)/shard_map/all_to_all | solution.py:67
  152.9 9.8 %collective-permute-done.10.refs_3_ = bf16[1024,512]{1,0:T(8,128)(2,1)S(1)} collective-permute-done((bf16[1024,512]{1,0:T(8,128)(2,1)}, bf16[1024,512]{1,0:T(8,128)(2,1)S(1)}, u32[]{:S(2)}, u32[]{:S(2)}) %collective-permute-start.10) | collective-permute-done | bytes 1048608 | tf_op jit(solution)/shard_map/ppermute | solution.py:50
  162.7 19.4 %prefix.1 = (f32[1088,128]{1,0:T(8,128)}, f32[1088,128]{1,0:T(8,128)}) custom-call(s32[1]{0:T(128)S(6)} %copy.33.count, bf16[1088,128]{1,0:T(8,128)(2,1)S(1)} %get-tuple-element.26.q_ref, bf16[2,1,16384,128]{3,2,1,0:T(8,128)(2,1)} %kv_ref.1), custom_call_target="tpu_custom_call" | custom-call | tf_op jit(solution)/shard_map/prefix/pallas_call | solution.py:353
  182.2 6.8 %finish.1 = bf16[8,8,136,128]{3,2,1,0:T(8,128)(2,1)} custom-call(bf16[1088,128]{1,0:T(8,128)(2,1)S(1)} %get-tuple-element.26.q_ref, f32[1088,128]{1,0:T(8,128)} %get-tuple-element.27.acc_in, f32[1088,128]{1,0:T(8,128)} %get-tuple-element.28.stat_in, bf16[16,136,256]{2,1,0:T(8,128)(2,1)S(1)} %all-to-all-done.3.kv), custom_call_target="tpu_custom_call" | custom-call | tf_op jit(solution)/shard_map/finish/pallas_call | solution.py:435
  189.0 36.4 %all_to_all.25.same = bf16[64,136,128]{2,1,0:T(8,128)(2,1)S(1)} all-to-all(bf16[64,136,128]{2,1,0:T(8,128)(2,1)} %bitcast.6), channel_id=1, replica_groups={{0,2,4,6,8,10,12,14,16,18,20,22,24,26,28,30,32,34,36,38,40,42,44,46,48,..., dimensions={0} | all-to-all | bytes 4456448 | tf_op jit(solution)/shard_map/all_to_all | solution.py:67
  226.7 2.0 collective-permute-start.13
  230.7 22.0 %collective-permute-done.12.refs_2_ = bf16[1024,512]{1,0:T(8,128)(2,1)S(1)} collective-permute-done((bf16[1024,512]{1,0:T(8,128)(2,1)S(1)}, bf16[1024,512]{1,0:T(8,128)(2,1)S(1)}, u32[]{:S(2)}, u32[]{:S(2)}) %collective-permute-start.12) | collective-permute-done | bytes 1048608 | tf_op jit(solution)/shard_map/ppermute | solution.py:50
  252.9 21.7 %collective-permute-done.14.refs_6_ = bf16[1024,512]{1,0:T(8,128)(2,1)S(1)} collective-permute-done((bf16[1024,512]{1,0:T(8,128)(2,1)}, bf16[1024,512]{1,0:T(8,128)(2,1)S(1)}, u32[]{:S(2)}, u32[]{:S(2)}) %collective-permute-start.14) | collective-permute-done | bytes 1048608 | tf_op jit(solution)/shard_map/ppermute | solution.py:50
  274.7 5.6 %output.1 = (bf16[256,512]{1,0:T(8,128)(2,1)}, bf16[8,2,512]{2,1,0:T(2,128)(2,1)}) custom-call(bf16[8,136,128]{2,1,0:T(8,128)(2,1)S(1)} %all-to-all-done.2.rest, bf16[64,136,128]{2,1,0:T(8,128)(2,1)S(1)} %all_to_all.25.same, bf16[64,136,128]{2,1,0:T(8,128)(2,1)S(1)} %collective-permute-done.11.crossed, bf16[1024,512]{1,0:T(8,128)(2,1)S(1)} %copy-done, ...), custom_call_target="tpu_custom_call" | custom-call | tf_op jit(solution)/shard_map/output/pallas_call | solution.py:507
  (54 shorter events, 18.2 us)
Async XLA Ops:
  1.4 0.9 copy-start.1
  15.4 9.9 %copy-start.2 = (bf16[512]{0:T(512)(128)(2,1)S(1)}, bf16[512]{0:T(512)(128)(2,1)}, u32[]{:S(2)}) copy-start(bf16[512]{0:T(512)(128)(2,1)} %param.14) | copy-start | bytes 3076
  15.4 38.5 %all-to-all-start = ((bf16[64,136,128]{2,1,0:T(8,128)(2,1)}), bf16[64,136,128]{2,1,0:T(8,128)(2,1)S(1)}, u32[]{:S(2)}, u32[]{:S(2)}) async-start(bf16[64,136,128]{2,1,0:T(8,128)(2,1)} %arrange.1), calls=%async_computation | async-start | bytes 4456448 | tf_op jit(solution)/shard_map/all_to_all | solution.py:67
  26.9 53.2 %collective-permute-start = (bf16[512,1280]{1,0:T(8,128)(2,1)S(1)}, bf16[512,1280]{1,0:T(8,128)(2,1)}, u32[]{:S(2)}, u32[]{:S(2)}) collective-permute-start(bf16[512,1280]{1,0:T(8,128)(2,1)S(1)} %multiply_convert_fusion.refs_0_), channel_id=1, source_target_pairs={{0,6},{1,7},{2,0},{3,1},{4,2},{5,3},{6,4},{7,5},{8,14},{9,15},{10,... | collective-permute-start | bytes 3932168 | tf_op jit(solution)/shard_map/ppermute | solution.py:59
  29.7 51.2 %collective-permute-start.1 = (bf16[512,1280]{1,0:T(8,128)(2,1)S(1)}, bf16[512,1280]{1,0:T(8,128)(2,1)}, u32[]{:S(2)}, u32[]{:S(2)}) collective-permute-start(bf16[512,1280]{1,0:T(8,128)(2,1)S(1)} %multiply_convert_fusion.refs_0_), channel_id=1, source_target_pairs={{0,2},{1,3},{2,4},{3,5},{4,6},{5,7},{6,0},{7,1},{8,10},{9,11},{10,... | collective-permute-start | bytes 3932168 | tf_op jit(solution)/shard_map/ppermute | solution.py:59
  56.9 52.5 %collective-permute-start.2 = (bf16[512,1280]{1,0:T(8,128)(2,1)S(1)}, bf16[512,1280]{1,0:T(8,128)(2,1)}, u32[]{:S(2)}, u32[]{:S(2)}) collective-permute-start(bf16[512,1280]{1,0:T(8,128)(2,1)S(1)} %multiply_convert_fusion.refs_0_), channel_id=1, source_target_pairs={{0,4},{1,5},{2,6},{3,7},{4,0},{5,1},{6,2},{7,3},{8,12},{9,13},{10,... | collective-permute-start | bytes 3932168 | tf_op jit(solution)/shard_map/ppermute | solution.py:59
  57.8 53.6 %collective-permute-start.3 = (bf16[512,1280]{1,0:T(8,128)(2,1)S(1)}, bf16[512,1280]{1,0:T(8,128)(2,1)}, u32[]{:S(2)}, u32[]{:S(2)}) collective-permute-start(bf16[512,1280]{1,0:T(8,128)(2,1)S(1)} %multiply_convert_fusion.refs_0_), channel_id=1, source_target_pairs={{0,1},{1,0},{2,3},{3,2},{4,5},{5,4},{6,7},{7,6},{8,9},{9,8},{10,11... | collective-permute-start | bytes 3932168 | tf_op jit(solution)/shard_map/ppermute | solution.py:54
  58.2 53.9 %all-to-all-start.1 = ((bf16[8,8,136,128]{3,2,1,0:T(8,128)(2,1)}), bf16[8,8,136,128]{3,2,1,0:T(8,128)(2,1)S(1)}, u32[]{:S(2)}, u32[]{:S(2)}) async-start(bf16[8,8,136,128]{3,2,1,0:T(8,128)(2,1)} %get-tuple-element.17), calls=%async_computation.1 | async-start | bytes 4456448 | tf_op jit(solution)/shard_map/all_to_all | solution.py:67
  80.1 31.9 %collective-permute-start.4 = (bf16[512,1280]{1,0:T(8,128)(2,1)}, bf16[512,1280]{1,0:T(8,128)(2,1)}, u32[]{:S(2)}, u32[]{:S(2)}) collective-permute-start(bf16[512,1280]{1,0:T(8,128)(2,1)} %collective-permute-done.refs_1_), channel_id=1, source_target_pairs={{0,1},{1,0},{2,3},{3,2},{4,5},{5,4},{6,7},{7,6},{8,9},{9,8},{10,11... | collective-permute-start | bytes 3932168 | tf_op jit(solution)/shard_map/ppermute | solution.py:54
  80.9 31.1 %collective-permute-start.5 = (bf16[512,1280]{1,0:T(8,128)(2,1)}, bf16[512,1280]{1,0:T(8,128)(2,1)}, u32[]{:S(2)}, u32[]{:S(2)}) collective-permute-start(bf16[512,1280]{1,0:T(8,128)(2,1)} %collective-permute-done.1.refs_2_), channel_id=1, source_target_pairs={{0,1},{1,0},{2,3},{3,2},{4,5},{5,4},{6,7},{7,6},{8,9},{9,8},{10,11... | collective-permute-start | bytes 3932168 | tf_op jit(solution)/shard_map/ppermute | solution.py:54
  109.3 3.4 %collective-permute-start.6 = (bf16[512,1280]{1,0:T(8,128)(2,1)}, bf16[512,1280]{1,0:T(8,128)(2,1)}, u32[]{:S(2)}, u32[]{:S(2)}) collective-permute-start(bf16[512,1280]{1,0:T(8,128)(2,1)} %collective-permute-done.2.refs_3_), channel_id=1, source_target_pairs={{0,1},{1,0},{2,3},{3,2},{4,5},{5,4},{6,7},{7,6},{8,9},{9,8},{10,11... | collective-permute-start | bytes 3932168 | tf_op jit(solution)/shard_map/ppermute | solution.py:54
  109.3 26.3 %collective-permute-start.8 = (bf16[1024,512]{1,0:T(8,128)(2,1)}, bf16[1024,512]{1,0:T(8,128)(2,1)}, u32[]{:S(2)}, u32[]{:S(2)}) collective-permute-start(bf16[1024,512]{1,0:T(8,128)(2,1)} %refs_0_.1), channel_id=1, source_target_pairs={{0,64},{16,80},{32,96},{48,112},{64,0},{80,16},{96,32},{112,48},{1... | collective-permute-start | bytes 3145736 | tf_op jit(solution)/shard_map/ppermute | solution.py:50
  111.4 25.6 %collective-permute-start.9 = (bf16[1024,512]{1,0:T(8,128)(2,1)}, bf16[1024,512]{1,0:T(8,128)(2,1)}, u32[]{:S(2)}, u32[]{:S(2)}) collective-permute-start(bf16[1024,512]{1,0:T(8,128)(2,1)} %refs_0_.1), channel_id=1, source_target_pairs={{0,16},{16,32},{32,48},{48,0},{64,80},{80,96},{96,112},{112,64},{1... | collective-permute-start | bytes 3145736 | tf_op jit(solution)/shard_map/ppermute | solution.py:50
  119.3 26.8 %collective-permute-start.7 = (bf16[136,1408]{1,0:T(8,128)(2,1)}, bf16[136,1408]{1,0:T(8,128)(2,1)S(1)}, u32[]{:S(2)}, u32[]{:S(2)}) collective-permute-start(bf16[136,1408]{1,0:T(8,128)(2,1)} %get-tuple-element.19), channel_id=1, source_target_pairs={{0,8},{1,9},{2,10},{3,11},{4,12},{5,13},{6,14},{7,15},{8,0},{9,1},... | collective-permute-start | bytes 1148936 | tf_op jit(solution)/shard_map/ppermute | solution.py:63
  122.3 15.2 %all-to-all-start.2 = ((bf16[8,136,128]{2,1,0:T(8,128)(2,1)}), bf16[8,136,128]{2,1,0:T(8,128)(2,1)S(1)}, u32[]{:S(2)}, u32[]{:S(2)}) async-start(bf16[8,136,128]{2,1,0:T(8,128)(2,1)} %get-tuple-element.20), calls=%async_computation.2 | async-start | bytes 557056 | tf_op jit(solution)/shard_map/all_to_all | solution.py:67
  136.9 25.8 %collective-permute-start.10 = (bf16[1024,512]{1,0:T(8,128)(2,1)}, bf16[1024,512]{1,0:T(8,128)(2,1)S(1)}, u32[]{:S(2)}, u32[]{:S(2)}) collective-permute-start(bf16[1024,512]{1,0:T(8,128)(2,1)} %collective-permute-done.8.refs_1_), channel_id=1, source_target_pairs={{0,48},{16,0},{32,16},{48,32},{64,112},{80,64},{96,80},{112,96},{1... | collective-permute-start | bytes 3145736 | tf_op jit(solution)/shard_map/ppermute | solution.py:50
  148.6 33.6 %all-to-all-start.3 = ((bf16[16,136,256]{2,1,0:T(8,128)(2,1)}), bf16[16,136,256]{2,1,0:T(8,128)(2,1)S(1)}, u32[]{:S(2)}, u32[]{:S(2)}) async-start(bf16[16,136,256]{2,1,0:T(8,128)(2,1)} %get-tuple-element.29), calls=%async_computation.3 | async-start | bytes 2228224 | tf_op jit(solution)/shard_map/all_to_all | solution.py:67
  189.0 36.4 %copy-start = (bf16[1024,512]{1,0:T(8,128)(2,1)S(1)}, bf16[1024,512]{1,0:T(8,128)(2,1)}, u32[]{:S(2)}) copy-start(bf16[1024,512]{1,0:T(8,128)(2,1)} %refs_0_.1) | copy-start | bytes 3145732
  225.4 49.3 %collective-permute-start.11 = (bf16[64,136,128]{2,1,0:T(8,128)(2,1)S(1)}, bf16[64,136,128]{2,1,0:T(8,128)(2,1)S(1)}, u32[]{:S(2)}, u32[]{:S(2)}) collective-permute-start(bf16[64,136,128]{2,1,0:T(8,128)(2,1)S(1)} %all_to_all.25.same), channel_id=1, source_target_pairs={{0,1},{1,0},{2,3},{3,2},{4,5},{5,4},{6,7},{7,6},{8,9},{9,8},{10,11... | collective-permute-start | bytes 6684680 | tf_op jit(solution)/shard_map/ppermute | solution.py:54
  225.4 27.2 %collective-permute-start.12 = (bf16[1024,512]{1,0:T(8,128)(2,1)S(1)}, bf16[1024,512]{1,0:T(8,128)(2,1)S(1)}, u32[]{:S(2)}, u32[]{:S(2)}) collective-permute-start(bf16[1024,512]{1,0:T(8,128)(2,1)S(1)} %copy-done), channel_id=1, source_target_pairs={{0,48},{16,0},{32,16},{48,32},{64,112},{80,64},{96,80},{112,96},{1... | collective-permute-start | bytes 3145736 | tf_op jit(solution)/shard_map/ppermute | solution.py:50
  226.7 26.2 %collective-permute-start.13 = (bf16[1024,512]{1,0:T(8,128)(2,1)}, bf16[1024,512]{1,0:T(8,128)(2,1)S(1)}, u32[]{:S(2)}, u32[]{:S(2)}) collective-permute-start(bf16[1024,512]{1,0:T(8,128)(2,1)} %collective-permute-done.8.refs_1_), channel_id=1, source_target_pairs={{0,16},{16,32},{32,48},{48,0},{64,80},{80,96},{96,112},{112,64},{1... | collective-permute-start | bytes 3145736 | tf_op jit(solution)/shard_map/ppermute | solution.py:50
  228.7 46.0 %collective-permute-start.14 = (bf16[1024,512]{1,0:T(8,128)(2,1)}, bf16[1024,512]{1,0:T(8,128)(2,1)S(1)}, u32[]{:S(2)}, u32[]{:S(2)}) collective-permute-start(bf16[1024,512]{1,0:T(8,128)(2,1)} %collective-permute-done.9.refs_4_), channel_id=1, source_target_pairs={{0,16},{16,32},{32,48},{48,0},{64,80},{80,96},{96,112},{112,64},{1... | collective-permute-start | bytes 3145736 | tf_op jit(solution)/shard_map/ppermute | solution.py:50
  229.7 45.0 %collective-permute-start.15 = (bf16[1024,512]{1,0:T(8,128)(2,1)S(1)}, bf16[1024,512]{1,0:T(8,128)(2,1)S(1)}, u32[]{:S(2)}, u32[]{:S(2)}) collective-permute-start(bf16[1024,512]{1,0:T(8,128)(2,1)S(1)} %collective-permute-done.10.refs_3_), channel_id=1, source_target_pairs={{0,48},{16,0},{32,16},{48,32},{64,112},{80,64},{96,80},{112,96},{1... | collective-permute-start | bytes 3145736 | tf_op jit(solution)/shard_map/ppermute | solution.py:50

commit v3 on v2

--- a/solution.py
+++ b/solution.py
@@ -449,38 +449,54 @@
     )(queries, *(in_hbm(block) for block in state), kv)
 
 
-def output_kernel(rest, same, crossed, *refs):
-    weights, (prompt_out, comp_out, matrix, sem) = refs[:SEQ], refs[SEQ:]
+def products(block, matrix, ready):
+    n = GROUPS * HEADS
+    order = selection(n, n, lambda r: r % GROUPS * HEADS + r // GROUPS)
+    seq = lax.axis_index("seq")
+    total = jnp.zeros((ROWS, matrix.shape[2]), jnp.float32)
+    for j in range(SEQ):
+        first = moved(seq, SHIFTS[j]) * GROUPS
+        left = []
+        for g in range(GROUPS):
+            parts = [block[first + g, pl.ds(16 * h, 16), :] for h in range(HEADS)]
+            left.append(jnp.concatenate(parts, axis=1))
+        comp = jnp.concatenate([block[first + g, PROMPT_ROWS:, :] for g in range(GROUPS)], axis=0)
+        comp = selected(order, comp)
+        parts = [comp[GROUPS * h : GROUPS * h + GROUPS] for h in range(HEADS)]
+        left.append(jnp.concatenate(parts, axis=1).astype(jnp.bfloat16))
+        left = jnp.concatenate(left, axis=0)
+        ready(j)
+        total = total + jnp.dot(left, matrix[j], preferred_element_type=jnp.float32)
+    return total
+
+
+def near_kernel(same, *refs):
+    weights, (total, matrix, sem) = refs[:SEQ], refs[SEQ:]
     loads = [pltpu.make_async_copy(w, matrix.at[j], sem.at[j]) for j, w in enumerate(weights)]
     for load in loads:
         load.start()
+    total[...] = products(same, matrix, lambda j: loads[j].wait())
+
+
+def near_output(same, weights):
+    depth, width = weights[0].shape
+    return pl.pallas_call(
+        near_kernel,
+        out_shape=(
+            jax.ShapeDtypeStruct((ROWS, width), jnp.float32),
+            pltpu.VMEM((SEQ, depth, width), jnp.bfloat16),
+        ),
+        in_specs=[whole()] + [whole(pl.ANY)] * SEQ,
+        out_specs=(whole(), whole()),
+        scratch_shapes=[pltpu.SemaphoreType.DMA((SEQ,))],
+        compiler_params=pltpu.CompilerParams(vmem_limit_bytes=18 << 20),
+        name="near_output",
+    )(same, *weights)
+
+
+def far_kernel(rest, crossed, near, matrix, prompt_out, comp_out):
     core = lax.axis_index("samp") % 2
-    seq = lax.axis_index("seq")
-    blocks = (same, crossed)
-    n = SAMP * HEADS
-
-    def comp_source(r):
-        head, token = r // SAMP, r % SAMP
-        group = token % 2 * 4 + token // 4
-        crossing = (token // 2 + core) % 2
-        return (crossing * GROUPS + group) * HEADS + head
-
-    order = selection(n, n, comp_source)
-    total = jnp.zeros((SAMP * 17, matrix.shape[2]), jnp.float32)
-    for j in range(SEQ):
-        first = moved(seq, SHIFTS[j]) * GROUPS
-        left = []
-        for b in blocks:
-            for g in range(GROUPS):
-                parts = [b[first + g, pl.ds(16 * h, 16), :] for h in range(HEADS)]
-                left.append(jnp.concatenate(parts, axis=1))
-        comp = [b[first + g, PROMPT_ROWS:, :] for b in blocks for g in range(GROUPS)]
-        comp = selected(order, jnp.concatenate(comp, axis=0)).astype(jnp.bfloat16)
-        parts = [comp[SAMP * h : SAMP * h + SAMP] for h in range(HEADS)]
-        left.append(jnp.concatenate(parts, axis=1))
-        left = jnp.concatenate(left, axis=0)
-        loads[j].wait()
-        total = total + jnp.dot(left, matrix[j], preferred_element_type=jnp.float32)
+    totals = (near[...], products(crossed, matrix, lambda j: None))
     for r in range(2):
         for g in range(GROUPS):
             slot = 2 * (g % 4) + (core + r) % 2
@@ -489,36 +505,39 @@
                 rest[slot, pl.ds(32 * k + 16 * (g // 4), 16), :].astype(jnp.float32)
                 for k in range(TILES)
             ]
-            i = 16 * (GROUPS * r + g)
             prompt_out[pl.ds(at, 16), :] = (
-                total[i : i + 16] + jnp.concatenate(parts, axis=1)
+                totals[r][16 * g : 16 * g + 16] + jnp.concatenate(parts, axis=1)
             ).astype(jnp.bfloat16)
     comp = jnp.concatenate([rest[f, PROMPT_ROWS:, :] for f in range(SLOTS)], axis=0)
+
+    def rest_of(r, k):
+        slot = 2 * (r % 4) + (r // GROUPS + core) % 2
+        return slot * 8 + 2 * k + r % GROUPS // 4
+
     parts = [
-        selected(selection(SAMP, 8 * SLOTS, lambda r: r // 2 * 8 + 2 * k + r % 2), comp)
-        for k in range(TILES)
+        selected(selection(SAMP, 8 * SLOTS, lambda r: rest_of(r, k)), comp) for k in range(TILES)
     ]
-    last = (total[2 * PROMPT_ROWS :] + jnp.concatenate(parts, axis=1)).astype(jnp.bfloat16)
-    comp_out[...] = last.reshape(comp_out.shape)
-
-
-def output(rest, same, crossed, weights):
-    width = weights[0].shape[1]
-    return pl.pallas_call(
-        output_kernel,
+    last = jnp.concatenate([t[PROMPT_ROWS:] for t in totals], axis=0)
+    last = (last + jnp.concatenate(parts, axis=1)).astype(jnp.bfloat16)
+    order = selection(
+        SAMP, SAMP, lambda r: (r // 2 + core) % 2 * GROUPS + r % 2 * 4 + r // 4
+    )
+    comp_out[...] = selected(order, last).astype(jnp.bfloat16).reshape(comp_out.shape)
+
+
+def far_output(rest, crossed, near, matrix):
+    width = near.shape[1]
+    return pl.pallas_call(
+        far_kernel,
         out_shape=(
             jax.ShapeDtypeStruct((2 * PROMPT_ROWS, width), jnp.bfloat16),
             jax.ShapeDtypeStruct((SAMP // 2, 2, width), jnp.bfloat16),
         ),
-        in_specs=[whole()] * 3 + [whole(pl.ANY)] * SEQ,
+        in_specs=[whole()] * 4,
         out_specs=(whole(), whole()),
-        scratch_shapes=[
-            pltpu.VMEM((SEQ, HEADS * HEAD, width), jnp.bfloat16),
-            pltpu.SemaphoreType.DMA((SEQ,)),
-        ],
-        compiler_params=pltpu.CompilerParams(vmem_limit_bytes=30 << 20),
-        name="output",
-    )(rest, same, crossed, *weights)
+        compiler_params=pltpu.CompilerParams(vmem_limit_bytes=22 << 20),
+        name="far_output",
+    )(rest, crossed, near, matrix)
 
 
 def body(
@@ -589,7 +608,8 @@
 
     same = exchange(context, ("seq", "samp"), SEQ_GROUP)
     crossed = to_other_core(same)
-    prompt_out, comp_out = output(rest, same, crossed, weights)
+    near, matrix = near_output(same, weights)
+    prompt_out, comp_out = far_output(rest, crossed, near, matrix)
     return prompt_out, comp_out
 
 

time: 285 us -> 285 us (level)
    pallas_call x1 -> x2, Pallas kernels: 5.57 us -> 6.65 us  [the longest x1 3.74 us: near_output(): pl.pallas_call(near_kernel, out_shape=(jax.ShapeDtypeStruct((ROWS, width)...]
  transfers between devices with their start and end apart: 20 -> 20, of which waited for: 12 -> 12; matrix products, arithmetic and copies ran while one was open for 3% -> 2% of each run, Pallas kernels for 11% -> 12%
where the time goes in v3:
time: 285 us; the launch traced here: 281 us
  waiting for transfers between devices  138 us (48%)
  Pallas kernels  46.3 us (16%)
  starting transfers between devices  37.9 us (13%)
  blocking collectives  36.4 us (13%)
  local copies, waits for them, and re-layouts  15.9 us (6%)
  other arithmetic  4.37 us (2%)
    ppermute x7, waiting for transfers between devices, to_seq(): lax.ppermute(block, 'seq', [(i, moved(i, shift)) for i in range(SEQ)])  64.6 us
    ppermute x3, waiting for transfers between devices, to_ring(): return lax.ppermute(block, 'samp', pairs)  45.2 us
    all_to_all x1, blocking collectives, exchange(): lax.all_to_all(blocks, axes, 0, 0, tiled=True, axis_index_groups=groups)  36.4 us
    all_to_all x4, starting transfers between devices, exchange(): lax.all_to_all(blocks, axes, 0, 0, tiled=True, axis_index_groups=groups)  23 us
    pallas_call x1, Pallas kernels, attend_prefix(): pl.pallas_call(functools.partial(prefix_kernel, slots=slots), out_shape=(...  19.4 us
    all_to_all x4, waiting for transfers between devices, exchange(): lax.all_to_all(blocks, axes, 0, 0, tiled=True, axis_index_groups=groups)  19.3 us
    gather x1, local copies, waits for them, and re-layouts, body(): picked = embed_table.at[local].get(mode='promise_in_bounds')  11.6 us
    ppermute x1, waiting for transfers between devices, to_other_pair(): lax.ppermute(block, 'samp', [(m, (m + 8) % SAMP) for m in range(SAMP)])  8.58 us
  transfers between devices with their start and end apart: 20, of which 12 were waited for; matrix products, arithmetic and copies ran while one was open for 2% of the time, Pallas kernels for 12%

profile of v3, /device:TPU:6, one launch (start us, length us, event | category | flops | bytes accessed | tf_op | source)
XLA Modules:
  0.0 281.4 jit_solution(3917023748874418002)
XLA Ops:
  2.3 11.6 %gather_fusion = bf16[2176,512]{1,0:T(8,128)(2,1)S(1)} fusion(bf16[8016,512]{1,0:T(8,128)(2,1)} %param.13, s32[3072]{0:T(1024)S(1)} %pad_clamp_fusion), kind=kCustom, calls=%fused_computation | custom fusion | bytes 4465152 | tf_op jit(solution)/shard_map/gather | solution.py:567
  15.4 9.9 %all-to-all-start = ((bf16[64,136,128]{2,1,0:T(8,128)(2,1)}), bf16[64,136,128]{2,1,0:T(8,128)(2,1)S(1)}, u32[]{:S(2)}, u32[]{:S(2)}) async-start(bf16[64,136,128]{2,1,0:T(8,128)(2,1)} %arrange.1), calls=%async_computation | async-start | bytes 4456448 | tf_op jit(solution)/shard_map/all_to_all | solution.py:67
  26.9 2.8 collective-permute-start
  34.7 19.3 %all-to-all-done.got = bf16[64,136,128]{2,1,0:T(8,128)(2,1)S(1)} async-done(((bf16[64,136,128]{2,1,0:T(8,128)(2,1)}), bf16[64,136,128]{2,1,0:T(8,128)(2,1)S(1)}, u32[]{:S(2)}, u32[]{:S(2)}) %all-to-all-start) | async-done | bytes 2228256 | tf_op jit(solution)/shard_map/all_to_all | solution.py:67
  54.0 2.9 %merge.1 = (bf16[8,8,136,128]{3,2,1,0:T(8,128)(2,1)}, bf16[8,136,128]{2,1,0:T(8,128)(2,1)}) custom-call(bf16[64,136,128]{2,1,0:T(8,128)(2,1)S(1)} %all-to-all-done.got, s32[136,1]{1,0:T(8,128)} %add_select_fusion.owners), custom_call_target="tpu_custom_call" | custom-call | tf_op jit(solution)/shard_map/merge/pallas_call | solution.py:147
  58.2 6.0 %all-to-all-start.1 = ((bf16[8,8,136,128]{3,2,1,0:T(8,128)(2,1)}), bf16[8,8,136,128]{3,2,1,0:T(8,128)(2,1)S(1)}, u32[]{:S(2)}, u32[]{:S(2)}) async-start(bf16[8,8,136,128]{3,2,1,0:T(8,128)(2,1)} %get-tuple-element.19), calls=%async_computation.1 | async-start | bytes 4456448 | tf_op jit(solution)/shard_map/all_to_all | solution.py:67
  64.2 16.0 %collective-permute-done.refs_1_ = bf16[512,1280]{1,0:T(8,128)(2,1)} collective-permute-done((bf16[512,1280]{1,0:T(8,128)(2,1)S(1)}, bf16[512,1280]{1,0:T(8,128)(2,1)}, u32[]{:S(2)}, u32[]{:S(2)}) %collective-permute-start) | collective-permute-done | bytes 1310752 | tf_op jit(solution)/shard_map/ppermute | solution.py:59
  80.9 28.4 %collective-permute-done.2.refs_3_ = bf16[512,1280]{1,0:T(8,128)(2,1)} collective-permute-done((bf16[512,1280]{1,0:T(8,128)(2,1)S(1)}, bf16[512,1280]{1,0:T(8,128)(2,1)}, u32[]{:S(2)}, u32[]{:S(2)}) %collective-permute-start.2) | collective-permute-done | bytes 1310752 | tf_op jit(solution)/shard_map/ppermute | solution.py:59
  109.4 2.0 collective-permute-start.8
  112.7 6.6 %project.1 = (bf16[136,1408]{1,0:T(8,128)(2,1)}, bf16[136,1408]{1,0:T(8,128)(2,1)}) custom-call(bf16[8,8,136,128]{3,2,1,0:T(8,128)(2,1)S(1)} %all-to-all-done.1.rows, bf16[512,1280]{1,0:T(8,128)(2,1)S(1)} %multiply_convert_fusion.refs_0_, bf16[512,1280]{1,0:T(8,128)(2,1)} %collective-permute-done.refs_1_, bf16[512,1280]{1,0:T(8,128)(2,1)} %collective-permute-done.1.refs_2_, ...), custom_call_target="tpu_custom_call" | custom-call | tf_op jit(solution)/shard_map/project/pallas_call | solution.py:226
  119.3 3.0 %collective-permute-start.7 = (bf16[136,1408]{1,0:T(8,128)(2,1)}, bf16[136,1408]{1,0:T(8,128)(2,1)S(1)}, u32[]{:S(2)}, u32[]{:S(2)}) collective-permute-start(bf16[136,1408]{1,0:T(8,128)(2,1)} %get-tuple-element.21), channel_id=1, source_target_pairs={{0,8},{1,9},{2,10},{3,11},{4,12},{5,13},{6,14},{7,15},{8,0},{9,1},... | collective-permute-start | bytes 1148936 | tf_op jit(solution)/shard_map/ppermute | solution.py:63
  122.4 3.4 %all-to-all-start.2 = ((bf16[8,136,128]{2,1,0:T(8,128)(2,1)}), bf16[8,136,128]{2,1,0:T(8,128)(2,1)S(1)}, u32[]{:S(2)}, u32[]{:S(2)}) async-start(bf16[8,136,128]{2,1,0:T(8,128)(2,1)} %get-tuple-element.22), calls=%async_computation.2 | async-start | bytes 557056 | tf_op jit(solution)/shard_map/all_to_all | solution.py:67
  126.1 9.6 %collective-permute-done.8.refs_1_ = bf16[1024,512]{1,0:T(8,128)(2,1)} collective-permute-done((bf16[1024,512]{1,0:T(8,128)(2,1)}, bf16[1024,512]{1,0:T(8,128)(2,1)}, u32[]{:S(2)}, u32[]{:S(2)}) %collective-permute-start.8) | collective-permute-done | bytes 1048608 | tf_op jit(solution)/shard_map/ppermute | solution.py:50
  137.6 8.6 %collective-permute-done.7.given = bf16[136,1408]{1,0:T(8,128)(2,1)S(1)} collective-permute-done((bf16[136,1408]{1,0:T(8,128)(2,1)}, bf16[136,1408]{1,0:T(8,128)(2,1)S(1)}, u32[]{:S(2)}, u32[]{:S(2)}) %collective-permute-start.7) | collective-permute-done | bytes 383008 | tf_op jit(solution)/shard_map/ppermute | solution.py:63
  146.2 2.4 rotate.1
  148.6 3.7 %all-to-all-start.3 = ((bf16[16,136,256]{2,1,0:T(8,128)(2,1)}), bf16[16,136,256]{2,1,0:T(8,128)(2,1)S(1)}, u32[]{:S(2)}, u32[]{:S(2)}) async-start(bf16[16,136,256]{2,1,0:T(8,128)(2,1)} %get-tuple-element.31), calls=%async_computation.3 | async-start | bytes 2228224 | tf_op jit(solution)/shard_map/all_to_all | solution.py:67
  153.0 9.8 %collective-permute-done.10.refs_3_ = bf16[1024,512]{1,0:T(8,128)(2,1)S(1)} collective-permute-done((bf16[1024,512]{1,0:T(8,128)(2,1)}, bf16[1024,512]{1,0:T(8,128)(2,1)S(1)}, u32[]{:S(2)}, u32[]{:S(2)}) %collective-permute-start.10) | collective-permute-done | bytes 1048608 | tf_op jit(solution)/shard_map/ppermute | solution.py:50
  162.7 19.4 %prefix.1 = (f32[1088,128]{1,0:T(8,128)}, f32[1088,128]{1,0:T(8,128)}) custom-call(s32[1]{0:T(128)S(6)} %copy.33.count, bf16[1088,128]{1,0:T(8,128)(2,1)S(1)} %get-tuple-element.28.q_ref, bf16[2,1,16384,128]{3,2,1,0:T(8,128)(2,1)} %kv_ref.1), custom_call_target="tpu_custom_call" | custom-call | tf_op jit(solution)/shard_map/prefix/pallas_call | solution.py:353
  182.2 6.8 %finish.1 = bf16[8,8,136,128]{3,2,1,0:T(8,128)(2,1)} custom-call(bf16[1088,128]{1,0:T(8,128)(2,1)S(1)} %get-tuple-element.28.q_ref, f32[1088,128]{1,0:T(8,128)} %get-tuple-element.29.acc_in, f32[1088,128]{1,0:T(8,128)} %get-tuple-element.30.stat_in, bf16[16,136,256]{2,1,0:T(8,128)(2,1)S(1)} %all-to-all-done.3.kv), custom_call_target="tpu_custom_call" | custom-call | tf_op jit(solution)/shard_map/finish/pallas_call | solution.py:435
  189.1 36.4 %all_to_all.25.same = bf16[64,136,128]{2,1,0:T(8,128)(2,1)S(1)} all-to-all(bf16[64,136,128]{2,1,0:T(8,128)(2,1)} %bitcast.6), channel_id=1, replica_groups={{0,2,4,6,8,10,12,14,16,18,20,22,24,26,28,30,32,34,36,38,40,42,44,46,48,..., dimensions={0} | all-to-all | bytes 4456448 | tf_op jit(solution)/shard_map/all_to_all | solution.py:67
  230.7 22.0 %collective-permute-done.12.refs_2_ = bf16[1024,512]{1,0:T(8,128)(2,1)S(1)} collective-permute-done((bf16[1024,512]{1,0:T(8,128)(2,1)S(1)}, bf16[1024,512]{1,0:T(8,128)(2,1)S(1)}, u32[]{:S(2)}, u32[]{:S(2)}) %collective-permute-start.12) | collective-permute-done | bytes 1048608 | tf_op jit(solution)/shard_map/ppermute | solution.py:50
  252.9 21.7 %collective-permute-done.14.refs_6_ = bf16[1024,512]{1,0:T(8,128)(2,1)S(1)} collective-permute-done((bf16[1024,512]{1,0:T(8,128)(2,1)}, bf16[1024,512]{1,0:T(8,128)(2,1)S(1)}, u32[]{:S(2)}, u32[]{:S(2)}) %collective-permute-start.14) | collective-permute-done | bytes 1048608 | tf_op jit(solution)/shard_map/ppermute | solution.py:50
  274.7 3.7 %near_output.1 = (f32[136,512]{1,0:T(8,128)S(1)}, bf16[8,1024,512]{2,1,0:T(8,128)(2,1)S(1)}) custom-call(bf16[64,136,128]{2,1,0:T(8,128)(2,1)S(1)} %all_to_all.25.same, bf16[1024,512]{1,0:T(8,128)(2,1)S(1)} %copy-done, bf16[1024,512]{1,0:T(8,128)(2,1)} %collective-permute-done.8.refs_1_, bf16[1024,512]{1,0:T(8,128)(2,1)S(1)} %collective-permute-done.12.refs_2_, ...), custom_call_target="tpu_custom_call" | custom-call | tf_op jit(solution)/shard_map/near_output/pallas_call | solution.py:483
  278.5 2.9 %far_output.1 = (bf16[256,512]{1,0:T(8,128)(2,1)}, bf16[8,2,512]{2,1,0:T(2,128)(2,1)}) custom-call(bf16[8,136,128]{2,1,0:T(8,128)(2,1)S(1)} %all-to-all-done.2.rest, bf16[64,136,128]{2,1,0:T(8,128)(2,1)S(1)} %collective-permute-done.11.crossed, f32[136,512]{1,0:T(8,128)S(1)} %get-tuple-element.34.near, bf16[8,1024,512]{2,1,0:T(8,128)(2,1)S(1)} %get-tuple-element.35.matrix), custom_call_target="tpu_custom_call" | custom-call | tf_op jit(solution)/shard_map/far_output/pallas_call | solution.py:530
  (55 shorter events, 20.2 us)
Async XLA Ops:
  1.4 0.9 copy-start.1
  15.4 9.9 %copy-start.2 = (bf16[512]{0:T(512)(128)(2,1)S(1)}, bf16[512]{0:T(512)(128)(2,1)}, u32[]{:S(2)}) copy-start(bf16[512]{0:T(512)(128)(2,1)} %param.14) | copy-start | bytes 3076
  15.4 38.5 %all-to-all-start = ((bf16[64,136,128]{2,1,0:T(8,128)(2,1)}), bf16[64,136,128]{2,1,0:T(8,128)(2,1)S(1)}, u32[]{:S(2)}, u32[]{:S(2)}) async-start(bf16[64,136,128]{2,1,0:T(8,128)(2,1)} %arrange.1), calls=%async_computation | async-start | bytes 4456448 | tf_op jit(solution)/shard_map/all_to_all | solution.py:67
  26.9 53.2 %collective-permute-start = (bf16[512,1280]{1,0:T(8,128)(2,1)S(1)}, bf16[512,1280]{1,0:T(8,128)(2,1)}, u32[]{:S(2)}, u32[]{:S(2)}) collective-permute-start(bf16[512,1280]{1,0:T(8,128)(2,1)S(1)} %multiply_convert_fusion.refs_0_), channel_id=1, source_target_pairs={{0,6},{1,7},{2,0},{3,1},{4,2},{5,3},{6,4},{7,5},{8,14},{9,15},{10,... | collective-permute-start | bytes 3932168 | tf_op jit(solution)/shard_map/ppermute | solution.py:59
  29.7 51.2 %collective-permute-start.1 = (bf16[512,1280]{1,0:T(8,128)(2,1)S(1)}, bf16[512,1280]{1,0:T(8,128)(2,1)}, u32[]{:S(2)}, u32[]{:S(2)}) collective-permute-start(bf16[512,1280]{1,0:T(8,128)(2,1)S(1)} %multiply_convert_fusion.refs_0_), channel_id=1, source_target_pairs={{0,2},{1,3},{2,4},{3,5},{4,6},{5,7},{6,0},{7,1},{8,10},{9,11},{10,... | collective-permute-start | bytes 3932168 | tf_op jit(solution)/shard_map/ppermute | solution.py:59
  56.9 52.4 %collective-permute-start.2 = (bf16[512,1280]{1,0:T(8,128)(2,1)S(1)}, bf16[512,1280]{1,0:T(8,128)(2,1)}, u32[]{:S(2)}, u32[]{:S(2)}) collective-permute-start(bf16[512,1280]{1,0:T(8,128)(2,1)S(1)} %multiply_convert_fusion.refs_0_), channel_id=1, source_target_pairs={{0,4},{1,5},{2,6},{3,7},{4,0},{5,1},{6,2},{7,3},{8,12},{9,13},{10,... | collective-permute-start | bytes 3932168 | tf_op jit(solution)/shard_map/ppermute | solution.py:59
  57.8 53.5 %collective-permute-start.3 = (bf16[512,1280]{1,0:T(8,128)(2,1)S(1)}, bf16[512,1280]{1,0:T(8,128)(2,1)}, u32[]{:S(2)}, u32[]{:S(2)}) collective-permute-start(bf16[512,1280]{1,0:T(8,128)(2,1)S(1)} %multiply_convert_fusion.refs_0_), channel_id=1, source_target_pairs={{0,1},{1,0},{2,3},{3,2},{4,5},{5,4},{6,7},{7,6},{8,9},{9,8},{10,11... | collective-permute-start | bytes 3932168 | tf_op jit(solution)/shard_map/ppermute | solution.py:54
  58.2 53.9 %all-to-all-start.1 = ((bf16[8,8,136,128]{3,2,1,0:T(8,128)(2,1)}), bf16[8,8,136,128]{3,2,1,0:T(8,128)(2,1)S(1)}, u32[]{:S(2)}, u32[]{:S(2)}) async-start(bf16[8,8,136,128]{3,2,1,0:T(8,128)(2,1)} %get-tuple-element.19), calls=%async_computation.1 | async-start | bytes 4456448 | tf_op jit(solution)/shard_map/all_to_all | solution.py:67
  80.2 31.9 %collective-permute-start.4 = (bf16[512,1280]{1,0:T(8,128)(2,1)}, bf16[512,1280]{1,0:T(8,128)(2,1)}, u32[]{:S(2)}, u32[]{:S(2)}) collective-permute-start(bf16[512,1280]{1,0:T(8,128)(2,1)} %collective-permute-done.refs_1_), channel_id=1, source_target_pairs={{0,1},{1,0},{2,3},{3,2},{4,5},{5,4},{6,7},{7,6},{8,9},{9,8},{10,11... | collective-permute-start | bytes 3932168 | tf_op jit(solution)/shard_map/ppermute | solution.py:54
  80.9 31.1 %collective-permute-start.5 = (bf16[512,1280]{1,0:T(8,128)(2,1)}, bf16[512,1280]{1,0:T(8,128)(2,1)}, u32[]{:S(2)}, u32[]{:S(2)}) collective-permute-start(bf16[512,1280]{1,0:T(8,128)(2,1)} %collective-permute-done.1.refs_2_), channel_id=1, source_target_pairs={{0,1},{1,0},{2,3},{3,2},{4,5},{5,4},{6,7},{7,6},{8,9},{9,8},{10,11... | collective-permute-start | bytes 3932168 | tf_op jit(solution)/shard_map/ppermute | solution.py:54
  109.4 3.4 %collective-permute-start.6 = (bf16[512,1280]{1,0:T(8,128)(2,1)}, bf16[512,1280]{1,0:T(8,128)(2,1)}, u32[]{:S(2)}, u32[]{:S(2)}) collective-permute-start(bf16[512,1280]{1,0:T(8,128)(2,1)} %collective-permute-done.2.refs_3_), channel_id=1, source_target_pairs={{0,1},{1,0},{2,3},{3,2},{4,5},{5,4},{6,7},{7,6},{8,9},{9,8},{10,11... | collective-permute-start | bytes 3932168 | tf_op jit(solution)/shard_map/ppermute | solution.py:54
  109.4 26.3 %collective-permute-start.8 = (bf16[1024,512]{1,0:T(8,128)(2,1)}, bf16[1024,512]{1,0:T(8,128)(2,1)}, u32[]{:S(2)}, u32[]{:S(2)}) collective-permute-start(bf16[1024,512]{1,0:T(8,128)(2,1)} %refs_0_.1), channel_id=1, source_target_pairs={{0,64},{16,80},{32,96},{48,112},{64,0},{80,16},{96,32},{112,48},{1... | collective-permute-start | bytes 3145736 | tf_op jit(solution)/shard_map/ppermute | solution.py:50
  111.4 25.6 %collective-permute-start.9 = (bf16[1024,512]{1,0:T(8,128)(2,1)}, bf16[1024,512]{1,0:T(8,128)(2,1)}, u32[]{:S(2)}, u32[]{:S(2)}) collective-permute-start(bf16[1024,512]{1,0:T(8,128)(2,1)} %refs_0_.1), channel_id=1, source_target_pairs={{0,16},{16,32},{32,48},{48,0},{64,80},{80,96},{96,112},{112,64},{1... | collective-permute-start | bytes 3145736 | tf_op jit(solution)/shard_map/ppermute | solution.py:50
  119.3 26.8 %collective-permute-start.7 = (bf16[136,1408]{1,0:T(8,128)(2,1)}, bf16[136,1408]{1,0:T(8,128)(2,1)S(1)}, u32[]{:S(2)}, u32[]{:S(2)}) collective-permute-start(bf16[136,1408]{1,0:T(8,128)(2,1)} %get-tuple-element.21), channel_id=1, source_target_pairs={{0,8},{1,9},{2,10},{3,11},{4,12},{5,13},{6,14},{7,15},{8,0},{9,1},... | collective-permute-start | bytes 1148936 | tf_op jit(solution)/shard_map/ppermute | solution.py:63
  122.4 15.2 %all-to-all-start.2 = ((bf16[8,136,128]{2,1,0:T(8,128)(2,1)}), bf16[8,136,128]{2,1,0:T(8,128)(2,1)S(1)}, u32[]{:S(2)}, u32[]{:S(2)}) async-start(bf16[8,136,128]{2,1,0:T(8,128)(2,1)} %get-tuple-element.22), calls=%async_computation.2 | async-start | bytes 557056 | tf_op jit(solution)/shard_map/all_to_all | solution.py:67
  136.9 25.8 %collective-permute-start.10 = (bf16[1024,512]{1,0:T(8,128)(2,1)}, bf16[1024,512]{1,0:T(8,128)(2,1)S(1)}, u32[]{:S(2)}, u32[]{:S(2)}) collective-permute-start(bf16[1024,512]{1,0:T(8,128)(2,1)} %collective-permute-done.8.refs_1_), channel_id=1, source_target_pairs={{0,48},{16,0},{32,16},{48,32},{64,112},{80,64},{96,80},{112,96},{1... | collective-permute-start | bytes 3145736 | tf_op jit(solution)/shard_map/ppermute | solution.py:50
  148.6 33.6 %all-to-all-start.3 = ((bf16[16,136,256]{2,1,0:T(8,128)(2,1)}), bf16[16,136,256]{2,1,0:T(8,128)(2,1)S(1)}, u32[]{:S(2)}, u32[]{:S(2)}) async-start(bf16[16,136,256]{2,1,0:T(8,128)(2,1)} %get-tuple-element.31), calls=%async_computation.3 | async-start | bytes 2228224 | tf_op jit(solution)/shard_map/all_to_all | solution.py:67
  189.1 36.4 %copy-start = (bf16[1024,512]{1,0:T(8,128)(2,1)S(1)}, bf16[1024,512]{1,0:T(8,128)(2,1)}, u32[]{:S(2)}) copy-start(bf16[1024,512]{1,0:T(8,128)(2,1)} %refs_0_.1) | copy-start | bytes 3145732
  225.4 53.0 %collective-permute-start.11 = (bf16[64,136,128]{2,1,0:T(8,128)(2,1)S(1)}, bf16[64,136,128]{2,1,0:T(8,128)(2,1)S(1)}, u32[]{:S(2)}, u32[]{:S(2)}) collective-permute-start(bf16[64,136,128]{2,1,0:T(8,128)(2,1)S(1)} %all_to_all.25.same), channel_id=1, source_target_pairs={{0,1},{1,0},{2,3},{3,2},{4,5},{5,4},{6,7},{7,6},{8,9},{9,8},{10,11... | collective-permute-start | bytes 6684680 | tf_op jit(solution)/shard_map/ppermute | solution.py:54
  225.4 27.2 %collective-permute-start.12 = (bf16[1024,512]{1,0:T(8,128)(2,1)S(1)}, bf16[1024,512]{1,0:T(8,128)(2,1)S(1)}, u32[]{:S(2)}, u32[]{:S(2)}) collective-permute-start(bf16[1024,512]{1,0:T(8,128)(2,1)S(1)} %copy-done), channel_id=1, source_target_pairs={{0,48},{16,0},{32,16},{48,32},{64,112},{80,64},{96,80},{112,96},{1... | collective-permute-start | bytes 3145736 | tf_op jit(solution)/shard_map/ppermute | solution.py:50
  226.7 26.2 %collective-permute-start.13 = (bf16[1024,512]{1,0:T(8,128)(2,1)}, bf16[1024,512]{1,0:T(8,128)(2,1)S(1)}, u32[]{:S(2)}, u32[]{:S(2)}) collective-permute-start(bf16[1024,512]{1,0:T(8,128)(2,1)} %collective-permute-done.8.refs_1_), channel_id=1, source_target_pairs={{0,16},{16,32},{32,48},{48,0},{64,80},{80,96},{96,112},{112,64},{1... | collective-permute-start | bytes 3145736 | tf_op jit(solution)/shard_map/ppermute | solution.py:50
  228.7 46.0 %collective-permute-start.14 = (bf16[1024,512]{1,0:T(8,128)(2,1)}, bf16[1024,512]{1,0:T(8,128)(2,1)S(1)}, u32[]{:S(2)}, u32[]{:S(2)}) collective-permute-start(bf16[1024,512]{1,0:T(8,128)(2,1)} %collective-permute-done.9.refs_4_), channel_id=1, source_target_pairs={{0,16},{16,32},{32,48},{48,0},{64,80},{80,96},{96,112},{112,64},{1... | collective-permute-start | bytes 3145736 | tf_op jit(solution)/shard_map/ppermute | solution.py:50
  229.7 45.0 %collective-permute-start.15 = (bf16[1024,512]{1,0:T(8,128)(2,1)S(1)}, bf16[1024,512]{1,0:T(8,128)(2,1)S(1)}, u32[]{:S(2)}, u32[]{:S(2)}) collective-permute-start(bf16[1024,512]{1,0:T(8,128)(2,1)S(1)} %collective-permute-done.10.refs_3_), channel_id=1, source_target_pairs={{0,48},{16,0},{32,16},{48,32},{64,112},{80,64},{96,80},{112,96},{1... | collective-permute-start | bytes 3145736 | tf_op jit(solution)/shard_map/ppermute | solution.py:50

commit v4 on v3

--- a/solution.py
+++ b/solution.py
@@ -299,11 +299,11 @@
 
     first = step * slots
 
-    def absorb(masked):
-        keys, values = kv_ref[0, 0], kv_ref[1, 0]
+    def absorb(masked, width):
+        keys, values = kv_ref[0, 0, :width, :], kv_ref[1, 0, :width, :]
         values = jnp.concatenate([values, jnp.ones_like(values)], axis=1)
         if masked:
-            ids = first + lax.broadcasted_iota(jnp.int32, (1, slots), 1)
+            ids = first + lax.broadcasted_iota(jnp.int32, (1, width), 1)
             bias = jnp.where(ids < count[0], 0.0, MASK_FILL)
         for h in range(HEADS):
             rows = pl.ds(h * ROWS, ROWS)
@@ -323,11 +323,15 @@
 
     @pl.when(first + slots <= count[0])
     def _():
-        absorb(False)
-
-    @pl.when((first < count[0]) & (first + slots > count[0]))
+        absorb(False, slots)
+
+    @pl.when((first + slots // 2 < count[0]) & (first + slots > count[0]))
     def _():
-        absorb(True)
+        absorb(True, slots)
+
+    @pl.when((first < count[0]) & (first + slots // 2 >= count[0]))
+    def _():
+        absorb(True, slots // 2)
 
     @pl.when(step == pl.num_programs(0) - 1)
     def _():

time: 285 us -> 284 us (level)
  transfers between devices with their start and end apart: 20 -> 20, of which waited for: 12 -> 12; matrix products, arithmetic and copies ran while one was open for 2% -> 3% of each run, Pallas kernels for 12% -> 12%
where the time goes in v4:
time: 284 us; the launch traced here: 280 us
  waiting for transfers between devices  138 us (49%)
  Pallas kernels  44.9 us (16%)
  starting transfers between devices  37.9 us (13%)
  blocking collectives  36.4 us (13%)
  local copies, waits for them, and re-layouts  15.9 us (6%)
  other arithmetic  4.37 us (2%)
    ppermute x7, waiting for transfers between devices, to_seq(): lax.ppermute(block, 'seq', [(i, moved(i, shift)) for i in range(SEQ)])  64.6 us
    ppermute x3, waiting for transfers between devices, to_ring(): return lax.ppermute(block, 'samp', pairs)  45.2 us
    all_to_all x1, blocking collectives, exchange(): lax.all_to_all(blocks, axes, 0, 0, tiled=True, axis_index_groups=groups)  36.4 us
    all_to_all x4, starting transfers between devices, exchange(): lax.all_to_all(blocks, axes, 0, 0, tiled=True, axis_index_groups=groups)  23 us
    all_to_all x4, waiting for transfers between devices, exchange(): lax.all_to_all(blocks, axes, 0, 0, tiled=True, axis_index_groups=groups)  19.3 us
    pallas_call x1, Pallas kernels, attend_prefix(): pl.pallas_call(functools.partial(prefix_kernel, slots=slots), out_shape=(...  18 us
    gather x1, local copies, waits for them, and re-layouts, body(): picked = embed_table.at[local].get(mode='promise_in_bounds')  11.6 us
    ppermute x1, waiting for transfers between devices, to_other_pair(): lax.ppermute(block, 'samp', [(m, (m + 8) % SAMP) for m in range(SAMP)])  8.58 us
  transfers between devices with their start and end apart: 20, of which 12 were waited for; matrix products, arithmetic and copies ran while one was open for 3% of the time, Pallas kernels for 12%

profile of v4, /device:TPU:6, one launch (start us, length us, event | category | flops | bytes accessed | tf_op | source)
XLA Modules:
  0.0 279.9 jit_solution(3230043344478054616)
XLA Ops:
  2.3 11.6 %gather_fusion = bf16[2176,512]{1,0:T(8,128)(2,1)S(1)} fusion(bf16[8016,512]{1,0:T(8,128)(2,1)} %param.13, s32[3072]{0:T(1024)S(1)} %pad_clamp_fusion), kind=kCustom, calls=%fused_computation | custom fusion | bytes 4465152 | tf_op jit(solution)/shard_map/gather | solution.py:571
  15.4 9.9 %all-to-all-start = ((bf16[64,136,128]{2,1,0:T(8,128)(2,1)}), bf16[64,136,128]{2,1,0:T(8,128)(2,1)S(1)}, u32[]{:S(2)}, u32[]{:S(2)}) async-start(bf16[64,136,128]{2,1,0:T(8,128)(2,1)} %arrange.1), calls=%async_computation | async-start | bytes 4456448 | tf_op jit(solution)/shard_map/all_to_all | solution.py:67
  26.9 2.8 collective-permute-start
  34.7 19.3 %all-to-all-done.got = bf16[64,136,128]{2,1,0:T(8,128)(2,1)S(1)} async-done(((bf16[64,136,128]{2,1,0:T(8,128)(2,1)}), bf16[64,136,128]{2,1,0:T(8,128)(2,1)S(1)}, u32[]{:S(2)}, u32[]{:S(2)}) %all-to-all-start) | async-done | bytes 2228256 | tf_op jit(solution)/shard_map/all_to_all | solution.py:67
  54.0 2.9 %merge.1 = (bf16[8,8,136,128]{3,2,1,0:T(8,128)(2,1)}, bf16[8,136,128]{2,1,0:T(8,128)(2,1)}) custom-call(bf16[64,136,128]{2,1,0:T(8,128)(2,1)S(1)} %all-to-all-done.got, s32[136,1]{1,0:T(8,128)} %add_select_fusion.owners), custom_call_target="tpu_custom_call" | custom-call | tf_op jit(solution)/shard_map/merge/pallas_call | solution.py:147
  58.2 6.0 %all-to-all-start.1 = ((bf16[8,8,136,128]{3,2,1,0:T(8,128)(2,1)}), bf16[8,8,136,128]{3,2,1,0:T(8,128)(2,1)S(1)}, u32[]{:S(2)}, u32[]{:S(2)}) async-start(bf16[8,8,136,128]{3,2,1,0:T(8,128)(2,1)} %get-tuple-element.19), calls=%async_computation.1 | async-start | bytes 4456448 | tf_op jit(solution)/shard_map/all_to_all | solution.py:67
  64.2 16.0 %collective-permute-done.refs_1_ = bf16[512,1280]{1,0:T(8,128)(2,1)} collective-permute-done((bf16[512,1280]{1,0:T(8,128)(2,1)S(1)}, bf16[512,1280]{1,0:T(8,128)(2,1)}, u32[]{:S(2)}, u32[]{:S(2)}) %collective-permute-start) | collective-permute-done | bytes 1310752 | tf_op jit(solution)/shard_map/ppermute | solution.py:59
  80.9 28.4 %collective-permute-done.2.refs_3_ = bf16[512,1280]{1,0:T(8,128)(2,1)} collective-permute-done((bf16[512,1280]{1,0:T(8,128)(2,1)S(1)}, bf16[512,1280]{1,0:T(8,128)(2,1)}, u32[]{:S(2)}, u32[]{:S(2)}) %collective-permute-start.2) | collective-permute-done | bytes 1310752 | tf_op jit(solution)/shard_map/ppermute | solution.py:59
  109.4 2.0 collective-permute-start.8
  112.7 6.6 %project.1 = (bf16[136,1408]{1,0:T(8,128)(2,1)}, bf16[136,1408]{1,0:T(8,128)(2,1)}) custom-call(bf16[8,8,136,128]{3,2,1,0:T(8,128)(2,1)S(1)} %all-to-all-done.1.rows, bf16[512,1280]{1,0:T(8,128)(2,1)S(1)} %multiply_convert_fusion.refs_0_, bf16[512,1280]{1,0:T(8,128)(2,1)} %collective-permute-done.refs_1_, bf16[512,1280]{1,0:T(8,128)(2,1)} %collective-permute-done.1.refs_2_, ...), custom_call_target="tpu_custom_call" | custom-call | tf_op jit(solution)/shard_map/project/pallas_call | solution.py:226
  119.3 3.0 %collective-permute-start.7 = (bf16[136,1408]{1,0:T(8,128)(2,1)}, bf16[136,1408]{1,0:T(8,128)(2,1)S(1)}, u32[]{:S(2)}, u32[]{:S(2)}) collective-permute-start(bf16[136,1408]{1,0:T(8,128)(2,1)} %get-tuple-element.21), channel_id=1, source_target_pairs={{0,8},{1,9},{2,10},{3,11},{4,12},{5,13},{6,14},{7,15},{8,0},{9,1},... | collective-permute-start | bytes 1148936 | tf_op jit(solution)/shard_map/ppermute | solution.py:63
  122.4 3.4 %all-to-all-start.2 = ((bf16[8,136,128]{2,1,0:T(8,128)(2,1)}), bf16[8,136,128]{2,1,0:T(8,128)(2,1)S(1)}, u32[]{:S(2)}, u32[]{:S(2)}) async-start(bf16[8,136,128]{2,1,0:T(8,128)(2,1)} %get-tuple-element.22), calls=%async_computation.2 | async-start | bytes 557056 | tf_op jit(solution)/shard_map/all_to_all | solution.py:67
  126.1 9.6 %collective-permute-done.8.refs_1_ = bf16[1024,512]{1,0:T(8,128)(2,1)} collective-permute-done((bf16[1024,512]{1,0:T(8,128)(2,1)}, bf16[1024,512]{1,0:T(8,128)(2,1)}, u32[]{:S(2)}, u32[]{:S(2)}) %collective-permute-start.8) | collective-permute-done | bytes 1048608 | tf_op jit(solution)/shard_map/ppermute | solution.py:50
  137.6 8.6 %collective-permute-done.7.given = bf16[136,1408]{1,0:T(8,128)(2,1)S(1)} collective-permute-done((bf16[136,1408]{1,0:T(8,128)(2,1)}, bf16[136,1408]{1,0:T(8,128)(2,1)S(1)}, u32[]{:S(2)}, u32[]{:S(2)}) %collective-permute-start.7) | collective-permute-done | bytes 383008 | tf_op jit(solution)/shard_map/ppermute | solution.py:63
  146.2 2.4 rotate.1
  148.6 3.7 %all-to-all-start.3 = ((bf16[16,136,256]{2,1,0:T(8,128)(2,1)}), bf16[16,136,256]{2,1,0:T(8,128)(2,1)S(1)}, u32[]{:S(2)}, u32[]{:S(2)}) async-start(bf16[16,136,256]{2,1,0:T(8,128)(2,1)} %get-tuple-element.31), calls=%async_computation.3 | async-start | bytes 2228224 | tf_op jit(solution)/shard_map/all_to_all | solution.py:67
  153.0 9.8 %collective-permute-done.10.refs_3_ = bf16[1024,512]{1,0:T(8,128)(2,1)S(1)} collective-permute-done((bf16[1024,512]{1,0:T(8,128)(2,1)}, bf16[1024,512]{1,0:T(8,128)(2,1)S(1)}, u32[]{:S(2)}, u32[]{:S(2)}) %collective-permute-start.10) | collective-permute-done | bytes 1048608 | tf_op jit(solution)/shard_map/ppermute | solution.py:50
  162.7 18.0 %prefix.1 = (f32[1088,128]{1,0:T(8,128)}, f32[1088,128]{1,0:T(8,128)}) custom-call(s32[1]{0:T(128)S(6)} %copy.33.count, bf16[1088,128]{1,0:T(8,128)(2,1)S(1)} %get-tuple-element.28.q_ref, bf16[2,1,16384,128]{3,2,1,0:T(8,128)(2,1)} %kv_ref.1), custom_call_target="tpu_custom_call" | custom-call | tf_op jit(solution)/shard_map/prefix/pallas_call | solution.py:357
  180.7 6.8 %finish.1 = bf16[8,8,136,128]{3,2,1,0:T(8,128)(2,1)} custom-call(bf16[1088,128]{1,0:T(8,128)(2,1)S(1)} %get-tuple-element.28.q_ref, f32[1088,128]{1,0:T(8,128)} %get-tuple-element.29.acc_in, f32[1088,128]{1,0:T(8,128)} %get-tuple-element.30.stat_in, bf16[16,136,256]{2,1,0:T(8,128)(2,1)S(1)} %all-to-all-done.3.kv), custom_call_target="tpu_custom_call" | custom-call | tf_op jit(solution)/shard_map/finish/pallas_call | solution.py:439
  187.6 36.4 %all_to_all.25.same = bf16[64,136,128]{2,1,0:T(8,128)(2,1)S(1)} all-to-all(bf16[64,136,128]{2,1,0:T(8,128)(2,1)} %bitcast.6), channel_id=1, replica_groups={{0,2,4,6,8,10,12,14,16,18,20,22,24,26,28,30,32,34,36,38,40,42,44,46,48,..., dimensions={0} | all-to-all | bytes 4456448 | tf_op jit(solution)/shard_map/all_to_all | solution.py:67
  229.2 22.0 %collective-permute-done.12.refs_2_ = bf16[1024,512]{1,0:T(8,128)(2,1)S(1)} collective-permute-done((bf16[1024,512]{1,0:T(8,128)(2,1)S(1)}, bf16[1024,512]{1,0:T(8,128)(2,1)S(1)}, u32[]{:S(2)}, u32[]{:S(2)}) %collective-permute-start.12) | collective-permute-done | bytes 1048608 | tf_op jit(solution)/shard_map/ppermute | solution.py:50
  251.4 21.7 %collective-permute-done.14.refs_6_ = bf16[1024,512]{1,0:T(8,128)(2,1)S(1)} collective-permute-done((bf16[1024,512]{1,0:T(8,128)(2,1)}, bf16[1024,512]{1,0:T(8,128)(2,1)S(1)}, u32[]{:S(2)}, u32[]{:S(2)}) %collective-permute-start.14) | collective-permute-done | bytes 1048608 | tf_op jit(solution)/shard_map/ppermute | solution.py:50
  273.2 3.7 %near_output.1 = (f32[136,512]{1,0:T(8,128)S(1)}, bf16[8,1024,512]{2,1,0:T(8,128)(2,1)S(1)}) custom-call(bf16[64,136,128]{2,1,0:T(8,128)(2,1)S(1)} %all_to_all.25.same, bf16[1024,512]{1,0:T(8,128)(2,1)S(1)} %copy-done, bf16[1024,512]{1,0:T(8,128)(2,1)} %collective-permute-done.8.refs_1_, bf16[1024,512]{1,0:T(8,128)(2,1)S(1)} %collective-permute-done.12.refs_2_, ...), custom_call_target="tpu_custom_call" | custom-call | tf_op jit(solution)/shard_map/near_output/pallas_call | solution.py:487
  277.0 2.9 %far_output.1 = (bf16[256,512]{1,0:T(8,128)(2,1)}, bf16[8,2,512]{2,1,0:T(2,128)(2,1)}) custom-call(bf16[8,136,128]{2,1,0:T(8,128)(2,1)S(1)} %all-to-all-done.2.rest, bf16[64,136,128]{2,1,0:T(8,128)(2,1)S(1)} %collective-permute-done.11.crossed, f32[136,512]{1,0:T(8,128)S(1)} %get-tuple-element.34.near, bf16[8,1024,512]{2,1,0:T(8,128)(2,1)S(1)} %get-tuple-element.35.matrix), custom_call_target="tpu_custom_call" | custom-call | tf_op jit(solution)/shard_map/far_output/pallas_call | solution.py:534
  (55 shorter events, 20.2 us)
Async XLA Ops:
  1.4 0.9 copy-start.1
  15.4 9.9 %copy-start.2 = (bf16[512]{0:T(512)(128)(2,1)S(1)}, bf16[512]{0:T(512)(128)(2,1)}, u32[]{:S(2)}) copy-start(bf16[512]{0:T(512)(128)(2,1)} %param.14) | copy-start | bytes 3076
  15.4 38.5 %all-to-all-start = ((bf16[64,136,128]{2,1,0:T(8,128)(2,1)}), bf16[64,136,128]{2,1,0:T(8,128)(2,1)S(1)}, u32[]{:S(2)}, u32[]{:S(2)}) async-start(bf16[64,136,128]{2,1,0:T(8,128)(2,1)} %arrange.1), calls=%async_computation | async-start | bytes 4456448 | tf_op jit(solution)/shard_map/all_to_all | solution.py:67
  26.9 53.2 %collective-permute-start = (bf16[512,1280]{1,0:T(8,128)(2,1)S(1)}, bf16[512,1280]{1,0:T(8,128)(2,1)}, u32[]{:S(2)}, u32[]{:S(2)}) collective-permute-start(bf16[512,1280]{1,0:T(8,128)(2,1)S(1)} %multiply_convert_fusion.refs_0_), channel_id=1, source_target_pairs={{0,6},{1,7},{2,0},{3,1},{4,2},{5,3},{6,4},{7,5},{8,14},{9,15},{10,... | collective-permute-start | bytes 3932168 | tf_op jit(solution)/shard_map/ppermute | solution.py:59
  29.7 51.2 %collective-permute-start.1 = (bf16[512,1280]{1,0:T(8,128)(2,1)S(1)}, bf16[512,1280]{1,0:T(8,128)(2,1)}, u32[]{:S(2)}, u32[]{:S(2)}) collective-permute-start(bf16[512,1280]{1,0:T(8,128)(2,1)S(1)} %multiply_convert_fusion.refs_0_), channel_id=1, source_target_pairs={{0,2},{1,3},{2,4},{3,5},{4,6},{5,7},{6,0},{7,1},{8,10},{9,11},{10,... | collective-permute-start | bytes 3932168 | tf_op jit(solution)/shard_map/ppermute | solution.py:59
  56.9 52.4 %collective-permute-start.2 = (bf16[512,1280]{1,0:T(8,128)(2,1)S(1)}, bf16[512,1280]{1,0:T(8,128)(2,1)}, u32[]{:S(2)}, u32[]{:S(2)}) collective-permute-start(bf16[512,1280]{1,0:T(8,128)(2,1)S(1)} %multiply_convert_fusion.refs_0_), channel_id=1, source_target_pairs={{0,4},{1,5},{2,6},{3,7},{4,0},{5,1},{6,2},{7,3},{8,12},{9,13},{10,... | collective-permute-start | bytes 3932168 | tf_op jit(solution)/shard_map/ppermute | solution.py:59
  57.8 53.5 %collective-permute-start.3 = (bf16[512,1280]{1,0:T(8,128)(2,1)S(1)}, bf16[512,1280]{1,0:T(8,128)(2,1)}, u32[]{:S(2)}, u32[]{:S(2)}) collective-permute-start(bf16[512,1280]{1,0:T(8,128)(2,1)S(1)} %multiply_convert_fusion.refs_0_), channel_id=1, source_target_pairs={{0,1},{1,0},{2,3},{3,2},{4,5},{5,4},{6,7},{7,6},{8,9},{9,8},{10,11... | collective-permute-start | bytes 3932168 | tf_op jit(solution)/shard_map/ppermute | solution.py:54
  58.2 53.9 %all-to-all-start.1 = ((bf16[8,8,136,128]{3,2,1,0:T(8,128)(2,1)}), bf16[8,8,136,128]{3,2,1,0:T(8,128)(2,1)S(1)}, u32[]{:S(2)}, u32[]{:S(2)}) async-start(bf16[8,8,136,128]{3,2,1,0:T(8,128)(2,1)} %get-tuple-element.19), calls=%async_computation.1 | async-start | bytes 4456448 | tf_op jit(solution)/shard_map/all_to_all | solution.py:67
  80.2 31.9 %collective-permute-start.4 = (bf16[512,1280]{1,0:T(8,128)(2,1)}, bf16[512,1280]{1,0:T(8,128)(2,1)}, u32[]{:S(2)}, u32[]{:S(2)}) collective-permute-start(bf16[512,1280]{1,0:T(8,128)(2,1)} %collective-permute-done.refs_1_), channel_id=1, source_target_pairs={{0,1},{1,0},{2,3},{3,2},{4,5},{5,4},{6,7},{7,6},{8,9},{9,8},{10,11... | collective-permute-start | bytes 3932168 | tf_op jit(solution)/shard_map/ppermute | solution.py:54
  80.9 31.1 %collective-permute-start.5 = (bf16[512,1280]{1,0:T(8,128)(2,1)}, bf16[512,1280]{1,0:T(8,128)(2,1)}, u32[]{:S(2)}, u32[]{:S(2)}) collective-permute-start(bf16[512,1280]{1,0:T(8,128)(2,1)} %collective-permute-done.1.refs_2_), channel_id=1, source_target_pairs={{0,1},{1,0},{2,3},{3,2},{4,5},{5,4},{6,7},{7,6},{8,9},{9,8},{10,11... | collective-permute-start | bytes 3932168 | tf_op jit(solution)/shard_map/ppermute | solution.py:54
  109.4 3.4 %collective-permute-start.6 = (bf16[512,1280]{1,0:T(8,128)(2,1)}, bf16[512,1280]{1,0:T(8,128)(2,1)}, u32[]{:S(2)}, u32[]{:S(2)}) collective-permute-start(bf16[512,1280]{1,0:T(8,128)(2,1)} %collective-permute-done.2.refs_3_), channel_id=1, source_target_pairs={{0,1},{1,0},{2,3},{3,2},{4,5},{5,4},{6,7},{7,6},{8,9},{9,8},{10,11... | collective-permute-start | bytes 3932168 | tf_op jit(solution)/shard_map/ppermute | solution.py:54
  109.4 26.3 %collective-permute-start.8 = (bf16[1024,512]{1,0:T(8,128)(2,1)}, bf16[1024,512]{1,0:T(8,128)(2,1)}, u32[]{:S(2)}, u32[]{:S(2)}) collective-permute-start(bf16[1024,512]{1,0:T(8,128)(2,1)} %refs_0_.1), channel_id=1, source_target_pairs={{0,64},{16,80},{32,96},{48,112},{64,0},{80,16},{96,32},{112,48},{1... | collective-permute-start | bytes 3145736 | tf_op jit(solution)/shard_map/ppermute | solution.py:50
  111.4 25.6 %collective-permute-start.9 = (bf16[1024,512]{1,0:T(8,128)(2,1)}, bf16[1024,512]{1,0:T(8,128)(2,1)}, u32[]{:S(2)}, u32[]{:S(2)}) collective-permute-start(bf16[1024,512]{1,0:T(8,128)(2,1)} %refs_0_.1), channel_id=1, source_target_pairs={{0,16},{16,32},{32,48},{48,0},{64,80},{80,96},{96,112},{112,64},{1... | collective-permute-start | bytes 3145736 | tf_op jit(solution)/shard_map/ppermute | solution.py:50
  119.3 26.8 %collective-permute-start.7 = (bf16[136,1408]{1,0:T(8,128)(2,1)}, bf16[136,1408]{1,0:T(8,128)(2,1)S(1)}, u32[]{:S(2)}, u32[]{:S(2)}) collective-permute-start(bf16[136,1408]{1,0:T(8,128)(2,1)} %get-tuple-element.21), channel_id=1, source_target_pairs={{0,8},{1,9},{2,10},{3,11},{4,12},{5,13},{6,14},{7,15},{8,0},{9,1},... | collective-permute-start | bytes 1148936 | tf_op jit(solution)/shard_map/ppermute | solution.py:63
  122.4 15.2 %all-to-all-start.2 = ((bf16[8,136,128]{2,1,0:T(8,128)(2,1)}), bf16[8,136,128]{2,1,0:T(8,128)(2,1)S(1)}, u32[]{:S(2)}, u32[]{:S(2)}) async-start(bf16[8,136,128]{2,1,0:T(8,128)(2,1)} %get-tuple-element.22), calls=%async_computation.2 | async-start | bytes 557056 | tf_op jit(solution)/shard_map/all_to_all | solution.py:67
  136.9 25.8 %collective-permute-start.10 = (bf16[1024,512]{1,0:T(8,128)(2,1)}, bf16[1024,512]{1,0:T(8,128)(2,1)S(1)}, u32[]{:S(2)}, u32[]{:S(2)}) collective-permute-start(bf16[1024,512]{1,0:T(8,128)(2,1)} %collective-permute-done.8.refs_1_), channel_id=1, source_target_pairs={{0,48},{16,0},{32,16},{48,32},{64,112},{80,64},{96,80},{112,96},{1... | collective-permute-start | bytes 3145736 | tf_op jit(solution)/shard_map/ppermute | solution.py:50
  148.6 32.1 %all-to-all-start.3 = ((bf16[16,136,256]{2,1,0:T(8,128)(2,1)}), bf16[16,136,256]{2,1,0:T(8,128)(2,1)S(1)}, u32[]{:S(2)}, u32[]{:S(2)}) async-start(bf16[16,136,256]{2,1,0:T(8,128)(2,1)} %get-tuple-element.31), calls=%async_computation.3 | async-start | bytes 2228224 | tf_op jit(solution)/shard_map/all_to_all | solution.py:67
  187.6 36.4 %copy-start = (bf16[1024,512]{1,0:T(8,128)(2,1)S(1)}, bf16[1024,512]{1,0:T(8,128)(2,1)}, u32[]{:S(2)}) copy-start(bf16[1024,512]{1,0:T(8,128)(2,1)} %refs_0_.1) | copy-start | bytes 3145732
  223.9 53.0 %collective-permute-start.11 = (bf16[64,136,128]{2,1,0:T(8,128)(2,1)S(1)}, bf16[64,136,128]{2,1,0:T(8,128)(2,1)S(1)}, u32[]{:S(2)}, u32[]{:S(2)}) collective-permute-start(bf16[64,136,128]{2,1,0:T(8,128)(2,1)S(1)} %all_to_all.25.same), channel_id=1, source_target_pairs={{0,1},{1,0},{2,3},{3,2},{4,5},{5,4},{6,7},{7,6},{8,9},{9,8},{10,11... | collective-permute-start | bytes 6684680 | tf_op jit(solution)/shard_map/ppermute | solution.py:54
  224.0 27.2 %collective-permute-start.12 = (bf16[1024,512]{1,0:T(8,128)(2,1)S(1)}, bf16[1024,512]{1,0:T(8,128)(2,1)S(1)}, u32[]{:S(2)}, u32[]{:S(2)}) collective-permute-start(bf16[1024,512]{1,0:T(8,128)(2,1)S(1)} %copy-done), channel_id=1, source_target_pairs={{0,48},{16,0},{32,16},{48,32},{64,112},{80,64},{96,80},{112,96},{1... | collective-permute-start | bytes 3145736 | tf_op jit(solution)/shard_map/ppermute | solution.py:50
  225.2 26.2 %collective-permute-start.13 = (bf16[1024,512]{1,0:T(8,128)(2,1)}, bf16[1024,512]{1,0:T(8,128)(2,1)S(1)}, u32[]{:S(2)}, u32[]{:S(2)}) collective-permute-start(bf16[1024,512]{1,0:T(8,128)(2,1)} %collective-permute-done.8.refs_1_), channel_id=1, source_target_pairs={{0,16},{16,32},{32,48},{48,0},{64,80},{80,96},{96,112},{112,64},{1... | collective-permute-start | bytes 3145736 | tf_op jit(solution)/shard_map/ppermute | solution.py:50
  227.2 46.0 %collective-permute-start.14 = (bf16[1024,512]{1,0:T(8,128)(2,1)}, bf16[1024,512]{1,0:T(8,128)(2,1)S(1)}, u32[]{:S(2)}, u32[]{:S(2)}) collective-permute-start(bf16[1024,512]{1,0:T(8,128)(2,1)} %collective-permute-done.9.refs_4_), channel_id=1, source_target_pairs={{0,16},{16,32},{32,48},{48,0},{64,80},{80,96},{96,112},{112,64},{1... | collective-permute-start | bytes 3145736 | tf_op jit(solution)/shard_map/ppermute | solution.py:50
  228.2 45.0 %collective-permute-start.15 = (bf16[1024,512]{1,0:T(8,128)(2,1)S(1)}, bf16[1024,512]{1,0:T(8,128)(2,1)S(1)}, u32[]{:S(2)}, u32[]{:S(2)}) collective-permute-start(bf16[1024,512]{1,0:T(8,128)(2,1)S(1)} %collective-permute-done.10.refs_3_), channel_id=1, source_target_pairs={{0,48},{16,0},{32,16},{48,32},{64,112},{80,64},{96,80},{112,96},{1... | collective-permute-start | bytes 3145736 | tf_op jit(solution)/shard_map/ppermute | solution.py:50
